TPU v7x, 128 devices: a whole 4x4x4 slice. The times are simulated.
128 devices in a mesh: rows: 32 (over z, y_lo, x), cols: 4 (over y_hi, core).
Axes of the slice: x: 4, y: 4 (y_hi: 2, y_lo: 2; y = y_hi * 2 + y_lo), z: 4, core: 2. Of those that a mesh axis runs over, the one named last changes fastest.
Arguments:
- field: bfloat16 [1, 18432, 18432], P(None, 'rows', 'cols'), may hold values from -48 to 48
Outputs:
- spectra: float32 [1, 1152, 2304], P(None, ('rows', 'cols'))
All inputs are finite; a program needn't handle non-finite values.
Results may differ from a plain program's by a relative error of at most 0.0003.
The roundings to bfloat16 on the way count: a program that leaves them out, or rounds other values in their place, can miss the bound.
Values may be sent and summed in bfloat16 or wider, within the bound.
A program may use at most 64 MiB of HBM per device.

v0:
```python
import math

import jax
import jax.numpy as jnp
from jax import lax
from jax.sharding import PartitionSpec as P

TAPS = 33
STRIDE = 8


def extended_2(shard, sides, width):
    for axis, dim in sides:
        count, length = (lax.axis_size(axis), shard.shape[dim])
        up = [(i, (i + 1) % count) for i in range(count - 1)]
        down = [(j, i) for i, j in up]
        last = lax.slice_in_dim(shard, length - width, length, axis=dim)
        initial = lax.slice_in_dim(shard, 0, width, axis=dim)
        before = lax.ppermute(last, axis, up)
        after = lax.ppermute(initial, axis, down)
        shard = jnp.concatenate([before, shard, after], axis=dim)
    return shard


def taps_table():
    tap_ids = jnp.arange(TAPS, dtype=jnp.float32)
    centre = TAPS // 2
    shaped = jnp.sinc((tap_ids - centre) / STRIDE) * (
        0.54 - 0.46 * jnp.cos(2 * jnp.pi * tap_ids / (TAPS - 1))
    )
    shaped = shaped / jnp.sum(shaped)
    rounded = lax.optimization_barrier(shaped.astype(jnp.bfloat16))
    return rounded.astype(jnp.float32)


def band_matrix(span_in, span_out, out_type):
    taps = taps_table()
    row_ids = lax.broadcasted_iota(jnp.int32, (span_in, span_out), 0)
    col_ids = lax.broadcasted_iota(jnp.int32, (span_in, span_out), 1)
    offset = row_ids - STRIDE * col_ids
    matrix = jnp.zeros((span_in, span_out), jnp.float32)
    for tap_id in range(TAPS):
        matrix = jnp.where(offset == tap_id, taps[tap_id], matrix)
    return matrix.astype(out_type)


def contract(form, left, right):
    if left.dtype == jnp.bfloat16:
        return jnp.einsum(form, left, right, preferred_element_type=jnp.float32)
    return jnp.einsum(form, left, right, precision=lax.Precision.HIGHEST)


def cut_along_rows(extended, count_out):
    matrix = band_matrix(extended.shape[1], count_out, extended.dtype)
    return contract("fic,io->foc", extended, matrix)


def cut_along_cols(extended, count_out):
    block_width = count_out // 4
    span_in = STRIDE * block_width + 2 * (TAPS // 2)
    matrix = band_matrix(span_in, block_width, extended.dtype)
    pieces = []
    for block_id in range(4):
        begin_at = STRIDE * block_width * block_id
        window = extended[:, :, begin_at : begin_at + span_in]
        pieces.append(contract("frc,co->fro", window, matrix))
    return jnp.concatenate(pieces, axis=2)


def weight_of(global_ids, length):
    return 0.5 - 0.5 * jnp.cos(2 * jnp.pi * global_ids.astype(jnp.float32) / length)


def angle_tables(point_ids, count_freq, length):
    freq_ids = lax.broadcasted_iota(jnp.int32, (point_ids.shape[0], count_freq), 1)
    reduced = point_ids[:, None] * freq_ids % length
    angles = 2 * jnp.pi / length * reduced.astype(jnp.float32)
    return (jnp.cos(angles), jnp.sin(angles))


def factor_of(length):
    factor_one = math.isqrt(length)
    while length % factor_one:
        factor_one = factor_one - 1
    return factor_one


def highest(form, left, right):
    return jnp.einsum(form, left, right, precision=lax.Precision.HIGHEST)


def dft_last(real_in, imag_in, length):
    factor_one = factor_of(length)
    factor_two = length // factor_one
    leading = real_in.shape[:-1]
    real_grid = real_in.reshape(leading + (factor_one, factor_two))
    cos_one, sin_one = angle_tables(jnp.arange(factor_one, dtype=jnp.int32), factor_one, factor_one)
    real_step = highest("...ab,ak->...kb", real_grid, cos_one)
    imag_step = -highest("...ab,ak->...kb", real_grid, sin_one)
    if imag_in is not None:
        imag_grid = imag_in.reshape(leading + (factor_one, factor_two))
        real_step = real_step + highest("...ab,ak->...kb", imag_grid, sin_one)
        imag_step = imag_step + highest("...ab,ak->...kb", imag_grid, cos_one)
    twiddle_cos, twiddle_sin = angle_tables(
        jnp.arange(factor_one, dtype=jnp.int32), factor_two, length
    )
    real_turned = real_step * twiddle_cos + imag_step * twiddle_sin
    imag_turned = imag_step * twiddle_cos - real_step * twiddle_sin
    cos_two, sin_two = angle_tables(jnp.arange(factor_two, dtype=jnp.int32), factor_two, factor_two)
    real_out = highest("...kb,bm->...mk", real_turned, cos_two) + highest(
        "...kb,bm->...mk", imag_turned, sin_two
    )
    imag_out = highest("...kb,bm->...mk", imag_turned, cos_two) - highest(
        "...kb,bm->...mk", real_turned, sin_two
    )
    return (real_out.reshape(leading + (length,)), imag_out.reshape(leading + (length,)))


def local(field):
    tap_reach = TAPS // 2
    row_devices = lax.axis_size("rows")
    raw_rows = field.shape[1]
    raw_cols = field.shape[2]
    out_rows = raw_rows // STRIDE
    out_cols = raw_cols // STRIDE
    length = out_rows * row_devices
    half_length = length // 2
    extended = extended_2(field, (("rows", 1),), tap_reach)
    rowcut = cut_along_rows(extended, out_rows)
    widened = extended_2(rowcut, (("cols", 2),), tap_reach)
    cut = cut_along_cols(widened, out_cols)
    row_global = lax.axis_index("rows") * out_rows + jnp.arange(out_rows, dtype=jnp.int32)
    col_global = lax.axis_index("cols") * out_cols + jnp.arange(out_cols, dtype=jnp.int32)
    tapered = (
        cut
        * weight_of(row_global, length)[None, :, None]
        * weight_of(col_global, length)[None, None, :]
    )
    grouped = lax.all_to_all(tapered, "cols", split_axis=1, concat_axis=2, tiled=True)
    real_col, imag_col = dft_last(grouped, None, length)
    partial_value = jnp.stack([real_col[..., :half_length], imag_col[..., :half_length]], axis=1)
    partial_value = jnp.swapaxes(partial_value, 2, 3)
    arrived = lax.all_to_all(
        partial_value, ("rows", "cols"), split_axis=2, concat_axis=3, tiled=True
    )
    real_row, imag_row = dft_last(arrived[:, 0], arrived[:, 1], length)
    return (real_row * real_row + imag_row * imag_row) * (8.0 / (length * length))


def solution(mesh):
    return jax.shard_map(
        local,
        mesh=mesh,
        in_specs=(P(None, "rows", "cols"),),
        out_specs=P(None, ("rows", "cols"), None),
        check_vma=False,
    )
```

profile of v0, /device:TPU:1, one launch (start us, length us, event | category | flops | bytes accessed | tf_op | source)
XLA Modules:
  0.0 197.2 jit_solution(8936054533083817620)
XLA Ops:
  0.0 1.0 fusion.479
  1.0 4.0 %collective-permute-start = (bf16[1,16,4608]{2,1,0:T(8,128)(2,1)S(1)}, bf16[1,16,4608]{2,1,0:T(8,128)(2,1)S(1)}, u32[]{:S(2)}, u32[]{:S(2)}) collective-permute-start(bf16[1,16,4608]{2,1,0:T(8,128)(2,1)S(1)} %get-tuple-element.8), channel_id=1, source_target_pairs={{0,4},{4,8},{8,12},{12,16},{16,20},{20,24},{24,28},{28,32},{32,36}... | collective-permute-start | bytes 442376 | tf_op jit(solution)/shard_map/ppermute | solution.py:19
  5.0 1.3 collective-permute-start.1
  9.2 2.1 %collective-permute-done.1 = bf16[1,16,4608]{2,1,0:T(8,128)(2,1)S(1)} collective-permute-done((bf16[1,16,4608]{2,1,0:T(8,128)(2,1)S(1)}, bf16[1,16,4608]{2,1,0:T(8,128)(2,1)S(1)}, u32[]{:S(2)}, u32[]{:S(2)}) %collective-permute-start.1) | collective-permute-done | bytes 147488 | tf_op jit(solution)/shard_map/ppermute | solution.py:20
  11.3 25.9 %convolution_bitcast_fusion = f32[1,72,4608]{2,1,0:T(8,128)S(1)} fusion(bf16[1,16,4608]{2,1,0:T(8,128)(2,1)S(1)} %collective-permute-done.1, bf16[1,576,4608]{2,1,0:T(8,128)(2,1)} %param.2, bf16[1,16,4608]{2,1,0:T(8,128)(2,1)S(1)} %collective-permute-done, f32[]{:T(128)} %bitcast.33, f32[]{:T(128)} %bitcast.32, f32[]{:T(128)} %bitcast.31, f32[]{:T(128)} %bitcast.30, ...), kind=kOutput, calls=%fused_computation | convolution fusion | flops 423182592 | bytes 6930852 | tf_op jit(solution)/shard_map/fic,io->foc/dot_general | solution.py:49
  37.2 24.1 %convolution_bitcast_fusion.3 = f32[1,72,144]{2,1,0:T(8,128)S(1)} fusion(f32[]{:T(128)} %bitcast.33, f32[]{:T(128)} %bitcast.32, f32[]{:T(128)} %bitcast.31, f32[]{:T(128)} %bitcast.30, f32[]{:T(128)} %bitcast.29, f32[]{:T(128)} %bitcast.28, f32[]{:T(128)} %bitcast.27, f32[]{:T(128)} %bitcast.26, f32[]{:T(128)} %bitcast.25, f32[]{:T(128)} %bitcast.24, ...), kind=kOutput, calls=%fused_computation.61 | convolution fusion | flops 158731776 | bytes 411268 | tf_op jit(solution)/shard_map/frc,co->fro/dot_general | solution.py:50
  61.3 6.6 %collective-permute-start.2 = (f32[1,72,16]{2,1,0:T(8,128)S(1)}, f32[1,72,16]{2,1,0:T(8,128)S(1)}, u32[]{:S(2)}, u32[]{:S(2)}) collective-permute-start(f32[1,72,16]{2,1,0:T(8,128)S(1)} %get-tuple-element.10), channel_id=1, source_target_pairs={{0,1},{1,2},{2,3},{4,5},{5,6},{6,7},{8,9},{9,10},{10,11},{12,13},{... | collective-permute-start | bytes 13832 | tf_op jit(solution)/shard_map/ppermute | solution.py:19
  67.9 24.1 %convolution_bitcast_fusion.4 = f32[1,72,144]{2,1,0:T(8,128)S(1)} fusion(f32[]{:T(128)} %bitcast.33, f32[]{:T(128)} %bitcast.32, f32[]{:T(128)} %bitcast.31, f32[]{:T(128)} %bitcast.30, f32[]{:T(128)} %bitcast.29, f32[]{:T(128)} %bitcast.28, f32[]{:T(128)} %bitcast.27, f32[]{:T(128)} %bitcast.26, f32[]{:T(128)} %bitcast.25, f32[]{:T(128)} %bitcast.24, ...), kind=kOutput, calls=%fused_computation.62 | convolution fusion | flops 158731776 | bytes 411268 | tf_op jit(solution)/shard_map/frc,co->fro/dot_general | solution.py:50
  92.0 2.1 %collective-permute-start.3 = (f32[1,72,16]{2,1,0:T(8,128)S(1)}, f32[1,72,16]{2,1,0:T(8,128)S(1)}, u32[]{:S(2)}, u32[]{:S(2)}) collective-permute-start(f32[1,72,16]{2,1,0:T(8,128)S(1)} %get-tuple-element.11), channel_id=1, source_target_pairs={{1,0},{2,1},{3,2},{5,4},{6,5},{7,6},{9,8},{10,9},{11,10},{13,12},{... | collective-permute-start | bytes 13832 | tf_op jit(solution)/shard_map/ppermute | solution.py:20
  94.1 24.1 %convolution_bitcast_fusion.5 = f32[1,72,144]{2,1,0:T(8,128)S(1)} fusion(f32[]{:T(128)} %bitcast.33, f32[]{:T(128)} %bitcast.32, f32[]{:T(128)} %bitcast.31, f32[]{:T(128)} %bitcast.30, f32[]{:T(128)} %bitcast.29, f32[]{:T(128)} %bitcast.28, f32[]{:T(128)} %bitcast.27, f32[]{:T(128)} %bitcast.26, f32[]{:T(128)} %bitcast.25, f32[]{:T(128)} %bitcast.24, ...), kind=kOutput, calls=%fused_computation.63 | convolution fusion | flops 158817024 | bytes 1373892 | tf_op jit(solution)/shard_map/frc,co->fro/dot_general | solution.py:50
  118.2 24.1 %convolution_bitcast_fusion.2 = f32[1,72,144]{2,1,0:T(8,128)S(1)} fusion(f32[]{:T(128)} %bitcast.33, f32[]{:T(128)} %bitcast.32, f32[]{:T(128)} %bitcast.31, f32[]{:T(128)} %bitcast.30, f32[]{:T(128)} %bitcast.29, f32[]{:T(128)} %bitcast.28, f32[]{:T(128)} %bitcast.27, f32[]{:T(128)} %bitcast.26, f32[]{:T(128)} %bitcast.25, f32[]{:T(128)} %bitcast.24, ...), kind=kOutput, calls=%fused_computation.60 | convolution fusion | flops 158817024 | bytes 1373892 | tf_op jit(solution)/shard_map/frc,co->fro/dot_general | solution.py:50
  143.2 4.9 %all-to-all-start = ((f32[1,72,576]{2,0,1:T(1,128)}), f32[1,72,576]{2,0,1:T(1,128)S(1)}, u32[]{:S(2)}, u32[]{:S(2)}) async-start(f32[1,72,576]{2,0,1:T(1,128)} %copy.24), calls=%async_computation | async-start | bytes 368640 | tf_op jit(solution)/shard_map/all_to_all | solution.py:139
  148.5 5.4 %all-to-all-done = f32[1,72,576]{2,0,1:T(1,128)S(1)} async-done(((f32[1,72,576]{2,0,1:T(1,128)}), f32[1,72,576]{2,0,1:T(1,128)S(1)}, u32[]{:S(2)}, u32[]{:S(2)}) %all-to-all-start) | async-done | bytes 165920 | tf_op jit(solution)/shard_map/all_to_all | solution.py:139
  155.6 1.7 fusion.50
  157.3 1.7 fusion.48
  159.0 1.7 fusion.5
  161.1 1.7 fusion.6
  164.2 1.2 reshape.314
  165.4 21.4 %all_to_all.33 = f32[128,1,324]{2,1,0:T(1,128)S(1)} all-to-all(f32[128,1,324]{2,1,0:T(1,128)S(1)} %reshape.314), channel_id=1, replica_groups=mesh['rows'=32,'cols'=4] {'rows','cols'}, dimensions={0} | all-to-all | bytes 331776 | tf_op jit(solution)/shard_map/all_to_all | solution.py:143
  187.3 1.1 reduce.4
  192.8 0.9 fusion.95
  193.7 0.9 fusion.93
  194.6 0.9 fusion.44
  195.5 0.9 fusion.43
  (39 shorter events, 13.4 us)
Async XLA Ops:
  1.0 8.2 %collective-permute-start = (bf16[1,16,4608]{2,1,0:T(8,128)(2,1)S(1)}, bf16[1,16,4608]{2,1,0:T(8,128)(2,1)S(1)}, u32[]{:S(2)}, u32[]{:S(2)}) collective-permute-start(bf16[1,16,4608]{2,1,0:T(8,128)(2,1)S(1)} %get-tuple-element.8), channel_id=1, source_target_pairs={{0,4},{4,8},{8,12},{12,16},{16,20},{20,24},{24,28},{28,32},{32,36}... | collective-permute-start | bytes 442376 | tf_op jit(solution)/shard_map/ppermute | solution.py:19
  5.0 6.3 %collective-permute-start.1 = (bf16[1,16,4608]{2,1,0:T(8,128)(2,1)S(1)}, bf16[1,16,4608]{2,1,0:T(8,128)(2,1)S(1)}, u32[]{:S(2)}, u32[]{:S(2)}) collective-permute-start(bf16[1,16,4608]{2,1,0:T(8,128)(2,1)S(1)} %get-tuple-element.9), channel_id=1, source_target_pairs={{4,0},{8,4},{12,8},{16,12},{20,16},{24,20},{28,24},{32,28},{36,32}... | collective-permute-start | bytes 442376 | tf_op jit(solution)/shard_map/ppermute | solution.py:20
  61.3 32.8 %collective-permute-start.2 = (f32[1,72,16]{2,1,0:T(8,128)S(1)}, f32[1,72,16]{2,1,0:T(8,128)S(1)}, u32[]{:S(2)}, u32[]{:S(2)}) collective-permute-start(f32[1,72,16]{2,1,0:T(8,128)S(1)} %get-tuple-element.10), channel_id=1, source_target_pairs={{0,1},{1,2},{2,3},{4,5},{5,6},{6,7},{8,9},{9,10},{10,11},{12,13},{... | collective-permute-start | bytes 13832 | tf_op jit(solution)/shard_map/ppermute | solution.py:19
  92.0 26.2 %collective-permute-start.3 = (f32[1,72,16]{2,1,0:T(8,128)S(1)}, f32[1,72,16]{2,1,0:T(8,128)S(1)}, u32[]{:S(2)}, u32[]{:S(2)}) collective-permute-start(f32[1,72,16]{2,1,0:T(8,128)S(1)} %get-tuple-element.11), channel_id=1, source_target_pairs={{1,0},{2,1},{3,2},{5,4},{6,5},{7,6},{9,8},{10,9},{11,10},{13,12},{... | collective-permute-start | bytes 13832 | tf_op jit(solution)/shard_map/ppermute | solution.py:20
  143.2 10.7 %all-to-all-start = ((f32[1,72,576]{2,0,1:T(1,128)}), f32[1,72,576]{2,0,1:T(1,128)S(1)}, u32[]{:S(2)}, u32[]{:S(2)}) async-start(f32[1,72,576]{2,0,1:T(1,128)} %copy.24), calls=%async_computation | async-start | bytes 368640 | tf_op jit(solution)/shard_map/all_to_all | solution.py:139
where the time goes:
time: 199 us; the launch traced here: 197 us
  matrix products  135 us (68%)
  blocking collectives  21.4 us (11%)
  starting transfers between devices  18.8 us (9%)
  local copies, waits for them, and re-layouts  10.5 us (5%)
  waiting for transfers between devices  7.55 us (4%)
  other arithmetic  3.09 us (2%)
    dot_general x4, matrix products, contract(): return jnp.einsum(form, left, right, precision=lax.Precision.HIGHEST)  96.2 us
    dot_general x1, matrix products, contract(): return jnp.einsum(form, left, right, preferred_element_type=jnp.float32)  25.9 us
    all_to_all x1, blocking collectives, local(): lax.all_to_all(partial_value, ('rows', 'cols'), split_axis=2, concat_axis...  21.4 us
    dot_general x14, matrix products, highest(): return jnp.einsum(form, left, right, precision=lax.Precision.HIGHEST)  13.3 us
    ppermute x2, starting transfers between devices, extended_2(): before = lax.ppermute(last, axis, up)  10.5 us
    all_to_all x1, waiting for transfers between devices, local(): lax.all_to_all(tapered, 'cols', split_axis=1, concat_axis=2, tiled=True)  5.45 us
    all_to_all x1, starting transfers between devices, local(): lax.all_to_all(tapered, 'cols', split_axis=1, concat_axis=2, tiled=True)  4.9 us
  transfers between devices with their start and end apart: 5, of which 2 were waited for; matrix products, arithmetic and copies ran while one was open for 26% of the time, Pallas kernels for 0%

commit v1 on v0

--- a/solution.py
+++ b/solution.py
@@ -3,6 +3,8 @@
 import jax
 import jax.numpy as jnp
 from jax import lax
+from jax.experimental import pallas as pl
+from jax.experimental.pallas import tpu as pltpu
 from jax.sharding import PartitionSpec as P
 
 TAPS = 33
@@ -114,6 +116,59 @@
         "...kb,bm->...mk", real_turned, sin_two
     )
     return (real_out.reshape(leading + (length,)), imag_out.reshape(leading + (length,)))
+
+
+def spread_kernel(src_ref, out_ref, got, filler, send_sem, recv_sem):
+    devices = got.shape[0]
+    cols = lax.axis_size("cols")
+    me = lax.axis_index("rows") * cols + lax.axis_index("cols")
+    barrier = pltpu.get_barrier_semaphore()
+
+    def place(step):
+        other = lax.rem(me + step, devices)
+        return other, (other // cols, lax.rem(other, cols))
+
+    @pl.loop(1, devices)
+    def _(step):
+        pl.semaphore_signal(
+            barrier, inc=1, device_id=place(step)[1], device_id_type=pl.DeviceIdType.MESH
+        )
+
+    pl.semaphore_wait(barrier, devices - 1)
+
+    @pl.loop(1, devices)
+    def _(step):
+        other, spot = place(step)
+        pltpu.make_async_remote_copy(
+            src_ref=src_ref.at[pl.ds(other, 1)],
+            dst_ref=got.at[pl.ds(me, 1)],
+            send_sem=send_sem,
+            recv_sem=recv_sem,
+            device_id=spot,
+            device_id_type=pl.DeviceIdType.MESH,
+        ).start()
+
+    pltpu.make_async_copy(filler, filler, recv_sem).wait()
+    pltpu.make_async_copy(filler, filler, send_sem).wait()
+    got[pl.ds(me, 1)] = src_ref[pl.ds(me, 1)]
+    out_ref[...] = got[...]
+
+
+def spread(blocks):
+    shape = blocks.shape
+    return pl.pallas_call(
+        spread_kernel,
+        out_shape=jax.ShapeDtypeStruct(shape, jnp.float32),
+        in_specs=[pl.BlockSpec(memory_space=pltpu.VMEM)],
+        out_specs=pl.BlockSpec(memory_space=pltpu.VMEM),
+        scratch_shapes=[
+            pltpu.VMEM(shape, jnp.float32),
+            pltpu.VMEM((shape[0] - 1,) + shape[1:], jnp.float32),
+            pltpu.SemaphoreType.DMA,
+            pltpu.SemaphoreType.DMA,
+        ],
+        compiler_params=pltpu.CompilerParams(collective_id=0, has_side_effects=True),
+    )(blocks)
 
 
 def local(field):
@@ -140,9 +195,14 @@
     real_col, imag_col = dft_last(grouped, None, length)
     partial_value = jnp.stack([real_col[..., :half_length], imag_col[..., :half_length]], axis=1)
     partial_value = jnp.swapaxes(partial_value, 2, 3)
-    arrived = lax.all_to_all(
-        partial_value, ("rows", "cols"), split_axis=2, concat_axis=3, tiled=True
-    )
+    devices = row_devices * lax.axis_size("cols")
+    blocks = partial_value.reshape(2, devices, half_length // devices, -1)
+    blocks = jnp.transpose(blocks, (1, 0, 2, 3)).reshape(devices, -1)
+    size = blocks.shape[1]
+    blocks = jnp.pad(blocks, ((0, 0), (0, -size % 128))).reshape(devices, -1, 128)
+    arrived = spread(blocks).reshape(devices, -1)[:, :size]
+    arrived = arrived.reshape(devices, 2, half_length // devices, -1)
+    arrived = jnp.transpose(arrived, (1, 2, 0, 3)).reshape(1, 2, half_length // devices, length)
     real_row, imag_row = dft_last(arrived[:, 0], arrived[:, 1], length)
     return (real_row * real_row + imag_row * imag_row) * (8.0 / (length * length))
 

time: 199 us -> 197 us (0.990)
  blocking collectives: 21.4 us -> 0 us
  Pallas kernels: 0 us -> 19.6 us
    all_to_all x1 -> x0, blocking collectives: 21.4 us -> none  [local(): lax.all_to_all(partial_value, ('rows', 'cols'), split_axis=2, concat_axis...]
    pallas_call x0 -> x1, Pallas kernels: none -> 19.6 us  [spread(): pl.pallas_call(spread_kernel, out_shape=jax.ShapeDtypeStruct(shape, jnp.f...]
    unnamed x2 -> x0, local copies, waits for them, and re-layouts: 2.05 us -> none
  transfers between devices with their start and end apart: 5 -> 5, of which waited for: 2 -> 2; matrix products, arithmetic and copies ran while one was open for 26% -> 39% of each run, Pallas kernels for 0% -> 0%
where the time goes in v1:
time: 197 us; the launch traced here: 195 us
  matrix products  135 us (69%)
  Pallas kernels  19.6 us (10%)
  starting transfers between devices  18.8 us (10%)
  local copies, waits for them, and re-layouts  11.2 us (6%)
  waiting for transfers between devices  7.54 us (4%)
  other arithmetic  1.98 us (1%)
    dot_general x4, matrix products, contract(): return jnp.einsum(form, left, right, precision=lax.Precision.HIGHEST)  96.2 us
    dot_general x1, matrix products, contract(): return jnp.einsum(form, left, right, preferred_element_type=jnp.float32)  25.9 us
    pallas_call x1, Pallas kernels, spread(): pl.pallas_call(spread_kernel, out_shape=jax.ShapeDtypeStruct(shape, jnp.f...  19.6 us
    dot_general x14, matrix products, highest(): return jnp.einsum(form, left, right, precision=lax.Precision.HIGHEST)  13.3 us
    ppermute x2, starting transfers between devices, extended_2(): before = lax.ppermute(last, axis, up)  10.5 us
    all_to_all x1, waiting for transfers between devices, local(): lax.all_to_all(tapered, 'cols', split_axis=1, concat_axis=2, tiled=True)  5.45 us
    all_to_all x1, starting transfers between devices, local(): lax.all_to_all(tapered, 'cols', split_axis=1, concat_axis=2, tiled=True)  4.9 us
  transfers between devices with their start and end apart: 5, of which 2 were waited for; matrix products, arithmetic and copies ran while one was open for 39% of the time, Pallas kernels for 0%

profile of v1, /device:TPU:1, one launch (start us, length us, event | category | flops | bytes accessed | tf_op | source)
XLA Modules:
  0.0 194.9 jit_solution(12994678387421430094)
XLA Ops:
  0.0 1.0 fusion.479
  1.0 4.0 %collective-permute-start = (bf16[1,16,4608]{2,1,0:T(8,128)(2,1)S(1)}, bf16[1,16,4608]{2,1,0:T(8,128)(2,1)S(1)}, u32[]{:S(2)}, u32[]{:S(2)}) collective-permute-start(bf16[1,16,4608]{2,1,0:T(8,128)(2,1)S(1)} %get-tuple-element.8), channel_id=1, source_target_pairs={{0,4},{4,8},{8,12},{12,16},{16,20},{20,24},{24,28},{28,32},{32,36}... | collective-permute-start | bytes 442376 | tf_op jit(solution)/shard_map/ppermute | solution.py:21
  5.0 1.3 collective-permute-start.1
  9.2 2.1 %collective-permute-done.1 = bf16[1,16,4608]{2,1,0:T(8,128)(2,1)S(1)} collective-permute-done((bf16[1,16,4608]{2,1,0:T(8,128)(2,1)S(1)}, bf16[1,16,4608]{2,1,0:T(8,128)(2,1)S(1)}, u32[]{:S(2)}, u32[]{:S(2)}) %collective-permute-start.1) | collective-permute-done | bytes 147488 | tf_op jit(solution)/shard_map/ppermute | solution.py:22
  11.3 25.9 %convolution_bitcast_fusion = f32[1,72,4608]{2,1,0:T(8,128)S(1)} fusion(bf16[1,16,4608]{2,1,0:T(8,128)(2,1)S(1)} %collective-permute-done.1, bf16[1,576,4608]{2,1,0:T(8,128)(2,1)} %param.2, bf16[1,16,4608]{2,1,0:T(8,128)(2,1)S(1)} %collective-permute-done, f32[]{:T(128)} %bitcast.33, f32[]{:T(128)} %bitcast.32, f32[]{:T(128)} %bitcast.31, f32[]{:T(128)} %bitcast.30, ...), kind=kOutput, calls=%fused_computation | convolution fusion | flops 423182592 | bytes 6930852 | tf_op jit(solution)/shard_map/fic,io->foc/dot_general | solution.py:51
  37.2 6.6 %collective-permute-start.2 = (f32[1,72,16]{2,1,0:T(8,128)S(1)}, f32[1,72,16]{2,1,0:T(8,128)S(1)}, u32[]{:S(2)}, u32[]{:S(2)}) collective-permute-start(f32[1,72,16]{2,1,0:T(8,128)S(1)} %get-tuple-element.10), channel_id=1, source_target_pairs={{0,1},{1,2},{2,3},{4,5},{5,6},{6,7},{8,9},{9,10},{10,11},{12,13},{... | collective-permute-start | bytes 13832 | tf_op jit(solution)/shard_map/ppermute | solution.py:21
  43.8 24.0 %convolution_bitcast_fusion.4 = f32[1,72,144]{2,1,0:T(8,128)S(1)} fusion(f32[]{:T(128)} %bitcast.33, f32[]{:T(128)} %bitcast.32, f32[]{:T(128)} %bitcast.31, f32[]{:T(128)} %bitcast.30, f32[]{:T(128)} %bitcast.29, f32[]{:T(128)} %bitcast.28, f32[]{:T(128)} %bitcast.27, f32[]{:T(128)} %bitcast.26, f32[]{:T(128)} %bitcast.25, f32[]{:T(128)} %bitcast.24, ...), kind=kOutput, calls=%fused_computation.62 | convolution fusion | flops 158731776 | bytes 411268 | tf_op jit(solution)/shard_map/frc,co->fro/dot_general | solution.py:52
  67.9 24.0 %convolution_bitcast_fusion.3 = f32[1,72,144]{2,1,0:T(8,128)S(1)} fusion(f32[]{:T(128)} %bitcast.33, f32[]{:T(128)} %bitcast.32, f32[]{:T(128)} %bitcast.31, f32[]{:T(128)} %bitcast.30, f32[]{:T(128)} %bitcast.29, f32[]{:T(128)} %bitcast.28, f32[]{:T(128)} %bitcast.27, f32[]{:T(128)} %bitcast.26, f32[]{:T(128)} %bitcast.25, f32[]{:T(128)} %bitcast.24, ...), kind=kOutput, calls=%fused_computation.61 | convolution fusion | flops 158731776 | bytes 411268 | tf_op jit(solution)/shard_map/frc,co->fro/dot_general | solution.py:52
  91.9 2.1 %collective-permute-start.3 = (f32[1,72,16]{2,1,0:T(8,128)S(1)}, f32[1,72,16]{2,1,0:T(8,128)S(1)}, u32[]{:S(2)}, u32[]{:S(2)}) collective-permute-start(f32[1,72,16]{2,1,0:T(8,128)S(1)} %get-tuple-element.11), channel_id=1, source_target_pairs={{1,0},{2,1},{3,2},{5,4},{6,5},{7,6},{9,8},{10,9},{11,10},{13,12},{... | collective-permute-start | bytes 13832 | tf_op jit(solution)/shard_map/ppermute | solution.py:22
  94.0 24.0 %convolution_bitcast_fusion.5 = f32[1,72,144]{2,1,0:T(8,128)S(1)} fusion(f32[]{:T(128)} %bitcast.33, f32[]{:T(128)} %bitcast.32, f32[]{:T(128)} %bitcast.31, f32[]{:T(128)} %bitcast.30, f32[]{:T(128)} %bitcast.29, f32[]{:T(128)} %bitcast.28, f32[]{:T(128)} %bitcast.27, f32[]{:T(128)} %bitcast.26, f32[]{:T(128)} %bitcast.25, f32[]{:T(128)} %bitcast.24, ...), kind=kOutput, calls=%fused_computation.63 | convolution fusion | flops 158817024 | bytes 1373892 | tf_op jit(solution)/shard_map/frc,co->fro/dot_general | solution.py:52
  118.1 24.0 %convolution_bitcast_fusion.2 = f32[1,72,144]{2,1,0:T(8,128)S(1)} fusion(f32[]{:T(128)} %bitcast.33, f32[]{:T(128)} %bitcast.32, f32[]{:T(128)} %bitcast.31, f32[]{:T(128)} %bitcast.30, f32[]{:T(128)} %bitcast.29, f32[]{:T(128)} %bitcast.28, f32[]{:T(128)} %bitcast.27, f32[]{:T(128)} %bitcast.26, f32[]{:T(128)} %bitcast.25, f32[]{:T(128)} %bitcast.24, ...), kind=kOutput, calls=%fused_computation.60 | convolution fusion | flops 158817024 | bytes 1373892 | tf_op jit(solution)/shard_map/frc,co->fro/dot_general | solution.py:52
  143.2 4.9 %all-to-all-start = ((f32[1,72,576]{2,0,1:T(1,128)}), f32[1,72,576]{2,0,1:T(1,128)S(1)}, u32[]{:S(2)}, u32[]{:S(2)}) async-start(f32[1,72,576]{2,0,1:T(1,128)} %copy.20), calls=%async_computation | async-start | bytes 368640 | tf_op jit(solution)/shard_map/all_to_all | solution.py:194
  148.4 5.4 %all-to-all-done = f32[1,72,576]{2,0,1:T(1,128)S(1)} async-done(((f32[1,72,576]{2,0,1:T(1,128)}), f32[1,72,576]{2,0,1:T(1,128)S(1)}, u32[]{:S(2)}, u32[]{:S(2)}) %all-to-all-start) | async-done | bytes 165920 | tf_op jit(solution)/shard_map/all_to_all | solution.py:194
  155.5 1.7 fusion.48
  157.2 1.7 fusion.50
  158.9 1.7 fusion.6
  161.0 1.7 fusion.5
  164.1 1.0 copy.25
  166.0 19.6 %shard_map.17 = f32[128,3,128]{2,1,0:T(4,128)} custom-call(f32[128,3,128]{2,1,0:T(4,128)} %copy.26.src_ref), custom_call_target="tpu_custom_call" | custom-call | tf_op jit(solution)/shard_map/pallas_call | solution.py:159
  185.6 1.1 copy.27
  190.5 0.9 fusion.95
  191.4 0.9 fusion.93
  192.3 0.9 fusion.44
  193.2 0.9 fusion.43
  (42 shorter events, 13.2 us)
Async XLA Ops:
  1.0 8.2 %collective-permute-start = (bf16[1,16,4608]{2,1,0:T(8,128)(2,1)S(1)}, bf16[1,16,4608]{2,1,0:T(8,128)(2,1)S(1)}, u32[]{:S(2)}, u32[]{:S(2)}) collective-permute-start(bf16[1,16,4608]{2,1,0:T(8,128)(2,1)S(1)} %get-tuple-element.8), channel_id=1, source_target_pairs={{0,4},{4,8},{8,12},{12,16},{16,20},{20,24},{24,28},{28,32},{32,36}... | collective-permute-start | bytes 442376 | tf_op jit(solution)/shard_map/ppermute | solution.py:21
  5.0 6.3 %collective-permute-start.1 = (bf16[1,16,4608]{2,1,0:T(8,128)(2,1)S(1)}, bf16[1,16,4608]{2,1,0:T(8,128)(2,1)S(1)}, u32[]{:S(2)}, u32[]{:S(2)}) collective-permute-start(bf16[1,16,4608]{2,1,0:T(8,128)(2,1)S(1)} %get-tuple-element.9), channel_id=1, source_target_pairs={{4,0},{8,4},{12,8},{16,12},{20,16},{24,20},{28,24},{32,28},{36,32}... | collective-permute-start | bytes 442376 | tf_op jit(solution)/shard_map/ppermute | solution.py:22
  37.2 56.8 %collective-permute-start.2 = (f32[1,72,16]{2,1,0:T(8,128)S(1)}, f32[1,72,16]{2,1,0:T(8,128)S(1)}, u32[]{:S(2)}, u32[]{:S(2)}) collective-permute-start(f32[1,72,16]{2,1,0:T(8,128)S(1)} %get-tuple-element.10), channel_id=1, source_target_pairs={{0,1},{1,2},{2,3},{4,5},{5,6},{6,7},{8,9},{9,10},{10,11},{12,13},{... | collective-permute-start | bytes 13832 | tf_op jit(solution)/shard_map/ppermute | solution.py:21
  91.9 26.2 %collective-permute-start.3 = (f32[1,72,16]{2,1,0:T(8,128)S(1)}, f32[1,72,16]{2,1,0:T(8,128)S(1)}, u32[]{:S(2)}, u32[]{:S(2)}) collective-permute-start(f32[1,72,16]{2,1,0:T(8,128)S(1)} %get-tuple-element.11), channel_id=1, source_target_pairs={{1,0},{2,1},{3,2},{5,4},{6,5},{7,6},{9,8},{10,9},{11,10},{13,12},{... | collective-permute-start | bytes 13832 | tf_op jit(solution)/shard_map/ppermute | solution.py:22
  143.2 10.7 %all-to-all-start = ((f32[1,72,576]{2,0,1:T(1,128)}), f32[1,72,576]{2,0,1:T(1,128)S(1)}, u32[]{:S(2)}, u32[]{:S(2)}) async-start(f32[1,72,576]{2,0,1:T(1,128)} %copy.20), calls=%async_computation | async-start | bytes 368640 | tf_op jit(solution)/shard_map/all_to_all | solution.py:194

commit v2 on v0

v2 whole, which is shorter than its diff:
```python
import jax
import jax.numpy as jnp
import ml_dtypes
import numpy as np
from jax import lax
from jax.experimental import pallas as pl
from jax.experimental.pallas import tpu as pltpu
from jax.sharding import PartitionSpec as P

TAPS = 33
STRIDE = 8
REACH = TAPS // 2
MESH = pl.DeviceIdType.MESH

ROWS, COLS = 32, 4
DEVICES = ROWS * COLS
LENGTH = 2304
RADIX = LENGTH // DEVICES
RAW_ROWS = LENGTH * STRIDE // ROWS
RAW_COLS = LENGTH * STRIDE // COLS
OUT_COLS = RAW_COLS // STRIDE
SLOT = 24
LANES = 128
WIDE = 5 * LANES
HALF = RADIX // 2


def taps_table():
    tap_ids = np.arange(TAPS, dtype=np.float32)
    shaped = np.sinc((tap_ids - np.float32(REACH)) / np.float32(STRIDE)).astype(np.float32)
    shaped = shaped * (
        np.float32(0.54)
        - np.float32(0.46) * np.cos(np.float32(2 * np.pi) * tap_ids / np.float32(TAPS - 1))
    )
    shaped = shaped / np.sum(shaped)
    return shaped.astype(ml_dtypes.bfloat16).astype(np.float32)


def tap_at(offset):
    taps = taps_table()
    inside = (offset >= 0) & (offset < TAPS)
    return np.where(inside, taps[np.clip(offset, 0, TAPS - 1)], 0).astype(ml_dtypes.bfloat16)


def split(matrix):
    high = matrix.astype(ml_dtypes.bfloat16)
    low = (matrix - high.astype(np.float64)).astype(ml_dtypes.bfloat16)
    return high, low


def tables():
    own = np.full((COLS, SLOT), -(10**6))
    own[:, :RADIX] = RADIX * np.arange(COLS)[:, None] + np.arange(RADIX)
    own[0, RADIX : RADIX + 2] = [-2, -1]
    own[-1, RADIX : RADIX + 2] = [COLS * RADIX, COLS * RADIX + 1]
    raw = np.arange(RAW_ROWS)
    row_band = tap_at(raw[None, :] - STRIDE * own.reshape(-1, 1) + REACH)

    lane = np.arange(LANES)
    inner = tap_at(np.arange(10 * LANES)[:, None] - LANES - STRIDE * lane[None, :] + REACH)
    edge = tap_at(lane[:, None] - STRIDE * (lane[None, :] - LANES) + REACH)
    col_band = np.concatenate([inner, edge], axis=0)

    angle = 2 * np.pi / LANES * (lane[:, None] * lane[None, :] % LANES)
    cos, sin = np.cos(angle), np.sin(angle)
    wave = np.block([[cos, -sin], [sin, cos]])
    first = np.concatenate([wave[:, : LANES // 2], wave[:, LANES : LANES + LANES // 2]], axis=1).T
    matrices = np.concatenate(split(first) + split(wave), axis=0)

    turn = 2 * np.pi / LENGTH * (np.arange(RADIX)[:, None] * lane[None, :])
    twiddles = np.stack([np.cos(turn), np.sin(turn)]).astype(np.float32)

    window = 0.5 - 0.5 * np.cos(2 * np.pi * np.arange(LENGTH) / LENGTH)
    row_window = np.zeros((DEVICES, SLOT))
    row_window[:, :RADIX] = window.reshape(DEVICES, RADIX)
    row_window = np.broadcast_to(row_window[:, :, None], (DEVICES, SLOT, LANES))
    col_window = np.broadcast_to(window[None, :], (8, LENGTH))
    return (
        row_band,
        col_band,
        matrices,
        twiddles,
        row_window.astype(np.float32),
        col_window.astype(np.float32),
    )


def real_nine(points):
    sums = [points[m] + points[9 - m] for m in range(1, 5)]
    gaps = [points[m] - points[9 - m] for m in range(1, 5)]
    reals, imags = [points[0] + sums[0] + sums[1] + sums[2] + sums[3]], [None]
    for freq in range(1, 5):
        real, imag = points[0], None
        for m in range(1, 5):
            phase = 2 * np.pi * (m * freq % 9) / 9
            real = real + sums[m - 1] * np.float32(np.cos(phase))
            term = gaps[m - 1] * np.float32(-np.sin(phase))
            imag = term if imag is None else imag + term
        reals.append(real)
        imags.append(imag)
    return reals, imags


def folded(points):
    evens = [points[2 * b % 18] for b in range(9)]
    odds = [points[(9 + 2 * b) % 18] for b in range(9)]
    return (
        real_nine([x + y for x, y in zip(evens, odds)]),
        real_nine([x - y for x, y in zip(evens, odds)]),
    )


def real_eighteen(points):
    both = folded(points)
    out = []
    for freq in range(18):
        reals, imags = both[freq % 2]
        at = freq % 9
        if at == 0:
            out.append((reals[0], None))
        elif at <= 4:
            out.append((reals[at], imags[at]))
        else:
            out.append((reals[9 - at], -imags[9 - at]))
    return out


def complex_eighteen(real_points, imag_points):
    both_real, both_imag = folded(real_points), folded(imag_points)
    out = []
    for freq in range(18):
        (a_re, a_im), (b_re, b_im) = both_real[freq % 2], both_imag[freq % 2]
        at = freq % 9
        if at == 0:
            out.append((a_re[0], b_re[0]))
        elif at <= 4:
            out.append((a_re[at] - b_im[at], a_im[at] + b_re[at]))
        else:
            out.append((a_re[9 - at] + b_im[9 - at], b_re[9 - at] - a_im[9 - at]))
    return out


def halves(value):
    high = value.astype(jnp.bfloat16)
    low = (value - high.astype(jnp.float32)).astype(jnp.bfloat16)
    return high, low


def product(left, right, dims):
    return lax.dot_general(left, right, (dims, ((), ())), preferred_element_type=jnp.float32)


def joined(blocks):
    lane = lax.broadcasted_iota(jnp.int32, (8, LANES), 1)
    turned = [pltpu.roll(b, 64, 1) if i % 2 else b for i, b in enumerate(blocks)]
    part = [[b[:, LANES * t : LANES * (t + 1)] for t in range(5)] for b in turned]
    zero = jnp.zeros((8, LANES), jnp.float32)
    out = part[0][:4]
    out.append(jnp.where(lane < 66, part[0][4], zero) + jnp.where(lane >= 62, part[1][0], zero))
    out += part[1][1:4]
    out.append(part[1][4] + jnp.where(lane >= 126, part[2][4], zero))
    out.append(part[2][0] + jnp.where(lane < 2, part[1][0], zero))
    out += part[2][1:4]
    out.append(jnp.where(lane < 66, part[2][4], zero) + jnp.where(lane >= 62, part[3][0], zero))
    out += part[3][1:5]
    return out


def kernel(
    field, row_band_in, col_band_in, matrices_in, twiddles_in, row_window_in, col_window_in,
    power,
    raw, row_band, col_band, matrices, twiddles, row_window, col_window,
    rowcut, cut, gathered, border, edges, turned, leaving, arrived, mixed, filler,
    load_sem, near_send, near_recv, edge_recv, far_send, far_recv,
):
    p, q = lax.axis_index("rows"), lax.axis_index("cols")
    me = p * COLS + q
    chunks = [(1024 * t, min(1024, RAW_COLS - 1024 * t)) for t in range(5)]
    loads = [
        pltpu.make_async_copy(row_band_in, row_band, load_sem.at[5]),
        pltpu.make_async_copy(col_band_in, col_band, load_sem.at[6]),
        pltpu.make_async_copy(matrices_in, matrices, load_sem.at[7]),
        pltpu.make_async_copy(twiddles_in, twiddles, load_sem.at[8]),
        pltpu.make_async_copy(row_window_in.at[me], row_window, load_sem.at[9]),
        pltpu.make_async_copy(col_window_in, col_window, load_sem.at[10]),
    ]
    field_loads = [
        pltpu.make_async_copy(
            field.at[0, :, pl.ds(begin, size)], raw.at[:, pl.ds(begin, size)], load_sem.at[t]
        )
        for t, (begin, size) in enumerate(chunks)
    ]
    for copy in loads[:1] + field_loads[:1] + loads[1:2] + field_loads[1:] + loads[2:]:
        copy.start()

    barrier = pltpu.get_barrier_semaphore()

    @pl.loop(1, DEVICES)
    def _(step):
        other = (me + step) & (DEVICES - 1)
        pl.semaphore_signal(
            barrier, inc=1, device_id=(other >> 2, other & 3), device_id_type=MESH
        )

    for row in (HALF * SLOT, 256 + HALF * SLOT):
        turned[pl.ds(row, 256 - HALF * SLOT), :] = jnp.zeros((256 - HALF * SLOT, 256), jnp.float32)
    edges[...] = jnp.zeros_like(edges)

    loads[0].wait()
    for t, (begin, size) in enumerate(chunks):
        field_loads[t].wait()
        if t == 1:
            loads[1].wait()
        part = product(row_band[...], raw[:, begin : begin + size], ((1,), (0,)))
        high, low = halves(part)
        rowcut[: COLS * SLOT, begin : begin + size] = high
        rowcut[COLS * SLOT :, begin : begin + size] = low
        blocks = [] if t == 0 else ([t - 1, t] if t == 4 else [t - 1])
        for u in blocks:
            lo, hi = max(1024 * u - LANES, 0), min(1024 * u + 1024 + LANES, RAW_COLS)
            skip = lo - (1024 * u - LANES)
            both = product(
                rowcut[:, lo:hi], col_band[skip : skip + hi - lo, :], ((1,), (0,))
            )
            if u == 4:
                both = both + product(
                    rowcut[:, :LANES], col_band[10 * LANES :, :], ((1,), (0,))
                )
            cut[:, LANES * u : LANES * (u + 1)] = both[: COLS * SLOT] + both[COLS * SLOT :]

    pl.semaphore_wait(barrier, DEVICES - 1)
    near = []
    for step in range(1, COLS):
        to = (q + step) & 3
        near.append(
            pltpu.make_async_remote_copy(
                src_ref=cut.at[pl.ds(pl.multiple_of(to * SLOT, 8), SLOT), :],
                dst_ref=gathered.at[q],
                send_sem=near_send.at[step - 1],
                recv_sem=near_recv.at[q],
                device_id=(p, to),
                device_id_type=MESH,
            )
        )
    for side, (row, to_p, to_q) in enumerate(
        ((3 * SLOT + 16, (p + 1) & 31, 3 * 0), (16, (p + 31) & 31, 3))
    ):
        near.append(
            pltpu.make_async_remote_copy(
                src_ref=cut.at[pl.ds(row, 8), :],
                dst_ref=border.at[q],
                send_sem=near_send.at[3 + side],
                recv_sem=edge_recv.at[q],
                device_id=(to_p, to_q),
                device_id_type=MESH,
            )
        )
    for copy in near:
        copy.start()
    gathered[q] = cut[pl.ds(pl.multiple_of(q * SLOT, 8), SLOT), :]
    for copy in loads[2:]:
        copy.wait()
    for step in range(1, COLS):
        source = (q + step) & 3
        pltpu.make_async_copy(
            gathered.at[source],
            gathered.at[source],
            near_recv.at[source],
        ).wait()

    row_id = lax.broadcasted_iota(jnp.int32, (8, LANES), 0)

    @pl.when((q == 0) | (q == 3))
    def _():
        for source in range(COLS):
            pltpu.make_async_copy(
                border.at[source], border.at[source], edge_recv.at[source]
            ).wait()
        valid = ((q == 0) & (p > 0)) | ((q == 3) & (p < ROWS - 1))
        keep = jnp.where(valid, 2, 0)
        for t, tile in enumerate(joined([border[source] for source in range(COLS)])):
            moved = pltpu.roll(tile, 6, 0)
            edges[:, LANES * t : LANES * (t + 1)] = jnp.where(row_id < keep, moved, 0.0)

    for s in range(3):
        rows = slice(8 * s, 8 * s + 8)
        points = joined([gathered[source, rows, :] for source in range(COLS)])
        if s == 2:
            points = [jnp.where(row_id < 2, x, 0.0) for x in points]
        if s != 1:
            flag = jnp.where(q == (0 if s == 0 else 3), 1.0, 0.0).astype(jnp.float32)
            points = [
                x + flag * edges[:, LANES * t : LANES * (t + 1)] for t, x in enumerate(points)
            ]
        points = [
            x * row_window[rows, :] * col_window[:, LANES * t : LANES * (t + 1)]
            for t, x in enumerate(points)
        ]
        for freq, (real, imag) in enumerate(real_eighteen(points)):
            at = (freq // HALF) * 256 + (freq % HALF) * SLOT + 8 * s
            cos, sin = twiddles[0, freq : freq + 1, :], twiddles[1, freq : freq + 1, :]
            if imag is None:
                turned[at : at + 8, :LANES] = real * cos
                turned[at : at + 8, LANES:] = -real * sin
            else:
                turned[at : at + 8, :LANES] = real * cos + imag * sin
                turned[at : at + 8, LANES:] = imag * cos - real * sin

    first_high, first_low = matrices[:LANES, :], matrices[LANES : 2 * LANES, :]
    for h in range(2):
        high, low = halves(turned[256 * h : 256 * (h + 1), :])
        both = (
            product(first_high, low, ((1,), (1,)))
            + product(first_low, high, ((1,), (1,)))
            + product(first_high, high, ((1,), (1,)))
        )
        leaving[0, :, 256 * h : 256 * (h + 1)] = both[: LANES // 2]
        leaving[1, :, 256 * h : 256 * (h + 1)] = both[LANES // 2 :]

    def block_of(other):
        lanes = pl.multiple_of((other & 1) * 256, 256)
        return leaving.at[:, pl.ds(other >> 1, 1), pl.ds(lanes, 256)]

    @pl.loop(1, DEVICES)
    def _(step):
        other = (me + step) & (DEVICES - 1)
        pltpu.make_async_remote_copy(
            src_ref=block_of(other),
            dst_ref=arrived.at[:, pl.ds(me, 1), :],
            send_sem=far_send,
            recv_sem=far_recv,
            device_id=(other >> 2, other & 3),
            device_id_type=MESH,
        ).start()

    pltpu.make_async_copy(block_of(me), arrived.at[:, pl.ds(me, 1), :], far_recv).start()
    pltpu.make_async_copy(arrived, arrived, far_recv).wait()

    wave_high, wave_low = matrices[2 * LANES : 4 * LANES, :], matrices[4 * LANES :, :]
    high, low = halves(arrived[...].reshape(2 * DEVICES, 256).T)
    both = (
        product(low, wave_high, ((1,), (0,)))
        + product(high, wave_low, ((1,), (0,)))
        + product(high, wave_high, ((1,), (0,)))
    )
    mixed[0], mixed[1] = both[:, :LANES], both[:, LANES:]
    real_points, imag_points = [], []
    for r in range(RADIX):
        real = mixed[0, pl.ds(r, HALF, stride=SLOT), :]
        imag = mixed[1, pl.ds(r, HALF, stride=SLOT), :]
        cos, sin = twiddles[0, r : r + 1, :], twiddles[1, r : r + 1, :]
        real_points.append(real * cos + imag * sin)
        imag_points.append(imag * cos - real * sin)
    for freq, (real, imag) in enumerate(complex_eighteen(real_points, imag_points)):
        power[:, LANES * freq : LANES * (freq + 1)] = (real * real + imag * imag) * np.float32(
            8.0 / (LENGTH * LENGTH)
        )

    for copy in near:
        copy.wait_send()
    pltpu.make_async_copy(filler, filler, far_send).wait()


def local(field):
    constants = tables()
    anywhere = pl.BlockSpec(memory_space=pltpu.HBM)
    f32, bf16 = jnp.float32, jnp.bfloat16
    power = pl.pallas_call(
        kernel,
        out_shape=jax.ShapeDtypeStruct((HALF, LENGTH), f32),
        in_specs=[anywhere] * (1 + len(constants)),
        out_specs=pl.BlockSpec(memory_space=pltpu.VMEM),
        scratch_shapes=[
            pltpu.VMEM((RAW_ROWS, RAW_COLS), bf16),
            pltpu.VMEM(constants[0].shape, bf16),
            pltpu.VMEM(constants[1].shape, bf16),
            pltpu.VMEM(constants[2].shape, bf16),
            pltpu.VMEM(constants[3].shape, f32),
            pltpu.VMEM((SLOT, LANES), f32),
            pltpu.VMEM(constants[5].shape, f32),
            pltpu.VMEM((2 * COLS * SLOT, RAW_COLS), bf16),
            pltpu.VMEM((COLS * SLOT, WIDE), f32),
            pltpu.VMEM((COLS, SLOT, WIDE), f32),
            pltpu.VMEM((COLS, 8, WIDE), f32),
            pltpu.VMEM((8, LENGTH), f32),
            pltpu.VMEM((512, 256), f32),
            pltpu.VMEM((2, LANES // 2, 512), f32),
            pltpu.VMEM((2, DEVICES, 256), f32),
            pltpu.VMEM((2, 256, LANES), f32),
            pltpu.VMEM((DEVICES - 1, 4, LANES), f32),
            pltpu.SemaphoreType.DMA((11,)),
            pltpu.SemaphoreType.DMA((5,)),
            pltpu.SemaphoreType.DMA((COLS,)),
            pltpu.SemaphoreType.DMA((COLS,)),
            pltpu.SemaphoreType.DMA,
            pltpu.SemaphoreType.DMA,
        ],
        compiler_params=pltpu.CompilerParams(
            collective_id=0, has_side_effects=True, vmem_limit_bytes=48 * 2**20
        ),
    )(field, *[jnp.asarray(c) for c in constants])
    return power[None]


def solution(mesh):
    return jax.shard_map(
        local,
        mesh=mesh,
        in_specs=(P(None, "rows", "cols"),),
        out_specs=P(None, ("rows", "cols"), None),
        check_vma=False,
    )
```

time: 199 us -> 31.8 us (0.16)
  matrix products: 135 us -> 0 us
  Pallas kernels: 0 us -> 24.9 us
  blocking collectives: 21.4 us -> 0 us
  starting transfers between devices: 18.8 us -> 0 us
  waiting for transfers between devices: 7.55 us -> 0 us
  local copies, waits for them, and re-layouts: 10.5 us -> 6.63 us
  other arithmetic: 3.09 us -> 0 us
    dot_general x19 -> x0, matrix products: 135 us -> none  [the longest x4 96.2 us: contract(): return jnp.einsum(form, left, right, precision=lax.Precision.HIGHEST)]
    pallas_call x0 -> x1, Pallas kernels: none -> 24.9 us  [local(): pl.pallas_call(kernel, out_shape=jax.ShapeDtypeStruct((HALF, LENGTH), f32...]
    all_to_all x1 -> x0, blocking collectives: 21.4 us -> none  [local(): lax.all_to_all(partial_value, ('rows', 'cols'), split_axis=2, concat_axis...]
    ppermute x4 -> x0, starting transfers between devices: 13.9 us -> none  [the longest x2 10.5 us: extended_2(): before = lax.ppermute(last, axis, up)]
    all_to_all x1 -> x0, waiting for transfers between devices: 5.45 us -> none  [local(): lax.all_to_all(tapered, 'cols', split_axis=1, concat_axis=2, tiled=True)]
    all_to_all x1 -> x0, starting transfers between devices: 4.9 us -> none  [local(): lax.all_to_all(tapered, 'cols', split_axis=1, concat_axis=2, tiled=True)]
    unnamed x2 -> x12, local copies, waits for them, and re-layouts: 2.05 us -> 5.91 us
    slice x5 -> x0, local copies, waits for them, and re-layouts: 2.95 us -> none  [the longest x2 1.45 us: band_matrix(): matrix = jnp.where(offset == tap_id, taps[tap_id], matrix)]
  transfers between devices with their start and end apart: 5 -> 0, of which waited for: 2 -> 0; matrix products, arithmetic and copies ran while one was open for 26% -> 0% of each run, Pallas kernels for 0% -> 0%
where the time goes in v2:
time: 31.8 us; the launch traced here: 31.5 us
  Pallas kernels  24.9 us (78%)
  local copies, waits for them, and re-layouts  6.63 us (21%)
    pallas_call x1, Pallas kernels, local(): pl.pallas_call(kernel, out_shape=jax.ShapeDtypeStruct((HALF, LENGTH), f32...  24.9 us
    unnamed x12, local copies, waits for them, and re-layouts  5.91 us
    broadcast_in_dim x1, local copies, waits for them, and re-layouts, local(): return power[None]  0.72 us

profile of v2, /device:TPU:1, one launch (start us, length us, event | category | flops | bytes accessed | tf_op | source)
XLA Modules:
  0.0 31.5 jit_solution(1708452555145363803)
XLA Ops:
  0.0 0.0 copy-start
  0.0 1.4 %copy-done = f32[128,24,128]{2,1,0:T(8,128)S(1)} copy-done((f32[128,24,128]{2,1,0:T(8,128)S(1)}, f32[128,24,128]{2,1,0:T(8,128)}, u32[]{:S(2)}) %copy-start) | copy-done | bytes 1572888
  1.4 0.0 copy-start.1
  1.4 1.0 %copy-done.1 = bf16[768,256]{1,0:T(8,128)(2,1)S(1)} copy-done((bf16[768,256]{1,0:T(8,128)(2,1)S(1)}, bf16[768,256]{1,0:T(8,128)(2,1)}, u32[]{:S(2)}) %copy-start.1) | copy-done | bytes 393240
  2.4 0.0 copy-start.2
  2.4 1.0 %copy-done.2 = bf16[1408,128]{1,0:T(8,128)(2,1)S(1)} copy-done((bf16[1408,128]{1,0:T(8,128)(2,1)S(1)}, bf16[1408,128]{1,0:T(8,128)(2,1)}, u32[]{:S(2)}) %copy-start.2) | copy-done | bytes 360472
  3.4 0.0 copy-start.3
  3.4 0.9 %copy-done.3 = bf16[96,576]{1,0:T(8,128)(2,1)S(1)} copy-done((bf16[96,576]{1,0:T(8,128)(2,1)S(1)}, bf16[96,576]{1,0:T(8,128)(2,1)}, u32[]{:S(2)}) %copy-start.3) | copy-done | bytes 110616
  4.3 0.0 copy-start.4
  4.3 0.9 %copy-done.4 = f32[8,2304]{1,0:T(8,128)S(1)} copy-done((f32[8,2304]{1,0:T(8,128)S(1)}, f32[8,2304]{1,0:T(8,128)}, u32[]{:S(2)}) %copy-start.4) | copy-done | bytes 73752
  5.2 0.0 copy-start.5
  5.2 0.7 %copy-done.5 = f32[2,18,128]{2,1,0:T(8,128)S(1)} copy-done((f32[2,18,128]{2,1,0:T(8,128)S(1)}, f32[2,18,128]{2,1,0:T(8,128)}, u32[]{:S(2)}) %copy-start.5) | copy-done | bytes 18456
  5.9 24.9 %shard_map.73 = f32[9,2304]{1,0:T(8,128)S(1)} custom-call(bf16[1,576,4608]{2,1,0:T(8,128)(2,1)} %field.1, bf16[96,576]{1,0:T(8,128)(2,1)S(1)} %copy-done.3, bf16[1408,128]{1,0:T(8,128)(2,1)S(1)} %copy-done.2, bf16[768,256]{1,0:T(8,128)(2,1)S(1)} %copy-done.1, f32[2,18,128]{2,1,0:T(8,128)S(1)} %copy-done.5, f32[128,24,128]{2,1,0:T(8,128)S(1)} %copy-done, ...), custom_call_target="tpu_custom_call" | custom-call | tf_op jit(solution)/shard_map/pallas_call | solution.py:368
  30.8 0.7 %copy.8 = f32[1,9,2304]{2,0,1:T(1,128)} copy(f32[1,9,2304]{2,1,0:T(8,128)S(1)} %bitcast.1) | data formatting | bytes 165888 | tf_op jit(solution)/shard_map/broadcast_in_dim | solution.py:402
Async XLA Ops:
  0.0 1.4 %copy-start = (f32[128,24,128]{2,1,0:T(8,128)S(1)}, f32[128,24,128]{2,1,0:T(8,128)}, u32[]{:S(2)}) copy-start(f32[128,24,128]{2,1,0:T(8,128)} %constant.16.clone.row_window_in) | copy-start | bytes 4718596
  1.4 1.0 %copy-start.1 = (bf16[768,256]{1,0:T(8,128)(2,1)S(1)}, bf16[768,256]{1,0:T(8,128)(2,1)}, u32[]{:S(2)}) copy-start(bf16[768,256]{1,0:T(8,128)(2,1)} %constant.14.clone.matrices_in) | copy-start | bytes 1179652
  2.4 1.0 %copy-start.2 = (bf16[1408,128]{1,0:T(8,128)(2,1)S(1)}, bf16[1408,128]{1,0:T(8,128)(2,1)}, u32[]{:S(2)}) copy-start(bf16[1408,128]{1,0:T(8,128)(2,1)} %constant.13.clone.col_band_in) | copy-start | bytes 1081348
  3.4 0.9 %copy-start.3 = (bf16[96,576]{1,0:T(8,128)(2,1)S(1)}, bf16[96,576]{1,0:T(8,128)(2,1)}, u32[]{:S(2)}) copy-start(bf16[96,576]{1,0:T(8,128)(2,1)} %constant.12.clone.row_band_in) | copy-start | bytes 331780
  4.3 0.9 %copy-start.4 = (f32[8,2304]{1,0:T(8,128)S(1)}, f32[8,2304]{1,0:T(8,128)}, u32[]{:S(2)}) copy-start(f32[8,2304]{1,0:T(8,128)} %constant.17.clone.col_window_in) | copy-start | bytes 221188
  5.2 0.7 %copy-start.5 = (f32[2,18,128]{2,1,0:T(8,128)S(1)}, f32[2,18,128]{2,1,0:T(8,128)}, u32[]{:S(2)}) copy-start(f32[2,18,128]{2,1,0:T(8,128)} %constant.15.clone.twiddles_in) | copy-start | bytes 55300

commit v3 on v2

--- a/solution.py
+++ b/solution.py
@@ -396,7 +396,7 @@
             pltpu.SemaphoreType.DMA,
         ],
         compiler_params=pltpu.CompilerParams(
-            collective_id=0, has_side_effects=True, vmem_limit_bytes=48 * 2**20
+            collective_id=0, has_side_effects=True, vmem_limit_bytes=56 * 2**20
         ),
     )(field, *[jnp.asarray(c) for c in constants])
     return power[None]

time: 31.8 us -> 26.7 us (0.84)
  local copies, waits for them, and re-layouts: 6.63 us -> 1.63 us
    unnamed x12 -> x0, local copies, waits for them, and re-layouts: 5.91 us -> none
    broadcast_in_dim x1, local copies, waits for them, and re-layouts: 0.72 us -> 1.63 us  [local(): return power[None]]
where the time goes in v3:
time: 26.7 us; the launch traced here: 26.6 us
  Pallas kernels  25 us (94%)
  local copies, waits for them, and re-layouts  1.63 us (6%)
    pallas_call x1, Pallas kernels, local(): pl.pallas_call(kernel, out_shape=jax.ShapeDtypeStruct((HALF, LENGTH), f32...  25 us
    broadcast_in_dim x1, local copies, waits for them, and re-layouts, local(): return power[None]  1.63 us

profile of v3, /device:TPU:1, one launch (start us, length us, event | category | flops | bytes accessed | tf_op | source)
XLA Modules:
  0.0 26.6 jit_solution(10672362247780843573)
XLA Ops:
  0.0 25.0 %shard_map.73 = f32[9,2304]{1,0:T(8,128)} custom-call(bf16[1,576,4608]{2,1,0:T(8,128)(2,1)} %field.1, bf16[96,576]{1,0:T(8,128)(2,1)} %constant.12.clone.row_band_in, bf16[1408,128]{1,0:T(8,128)(2,1)} %constant.13.clone.col_band_in, bf16[768,256]{1,0:T(8,128)(2,1)} %constant.14.clone.matrices_in, f32[2,18,128]{2,1,0:T(8,128)} %constant.15.clone.twiddles_in, ...), custom_call_target="tpu_custom_call" | custom-call | tf_op jit(solution)/shard_map/pallas_call | solution.py:368
  25.0 1.6 %copy.8 = f32[1,9,2304]{2,0,1:T(1,128)} copy(f32[1,9,2304]{2,1,0:T(8,128)} %bitcast.1) | data formatting | bytes 165888 | tf_op jit(solution)/shard_map/broadcast_in_dim | solution.py:402

commit v4 on v3

--- a/solution.py
+++ b/solution.py
@@ -25,6 +25,14 @@
 HALF = RADIX // 2
 
 
+FARTHEST = 74
+GROUP_A = [1, 2, 3]
+GROUP_B = [4 * k for k in range(1, 8)]
+GROUP_C = [32, 64, 96]
+CUTS = [0, 640] + [640 + 512 * t for t in range(1, 8)] + [RAW_COLS]
+CHUNKS = list(zip(CUTS[:-1], CUTS[1:]))
+
+
 def taps_table():
     tap_ids = np.arange(TAPS, dtype=np.float32)
     shaped = np.sinc((tap_ids - np.float32(REACH)) / np.float32(STRIDE)).astype(np.float32)
@@ -74,15 +82,11 @@
     row_window = np.zeros((DEVICES, SLOT))
     row_window[:, :RADIX] = window.reshape(DEVICES, RADIX)
     row_window = np.broadcast_to(row_window[:, :, None], (DEVICES, SLOT, LANES))
-    col_window = np.broadcast_to(window[None, :], (8, LENGTH))
-    return (
-        row_band,
-        col_band,
-        matrices,
-        twiddles,
-        row_window.astype(np.float32),
-        col_window.astype(np.float32),
-    )
+    col_window = np.broadcast_to(window.reshape(RADIX, 1, LANES), (RADIX, 8, LANES))
+    twiddles = np.pad(twiddles, ((0, 0), (0, SLOT - RADIX), (0, 0)))
+    floats = np.concatenate([row_window, twiddles, col_window.reshape(-1, SLOT, LANES)], axis=0)
+    row_band = np.pad(row_band, ((0, COLS * SLOT), (0, WIDE - RAW_ROWS)))
+    return row_band, col_band, matrices, floats.astype(np.float32)
 
 
 def real_nine(points):
@@ -167,120 +171,136 @@
 
 
 def kernel(
-    field, row_band_in, col_band_in, matrices_in, twiddles_in, row_window_in, col_window_in,
+    field, row_band_in, col_band_in, matrices_in, floats_in,
     power,
-    raw, row_band, col_band, matrices, twiddles, row_window, col_window,
+    raw, row_band, col_band, matrices, common, row_window,
     rowcut, cut, gathered, border, edges, turned, leaving, arrived, mixed, filler,
-    load_sem, near_send, near_recv, edge_recv, far_send, far_recv,
+    load_sem, near_send, near_recv, edge_send, edge_recv, far_send, far_recv, group_ready, all_ready,
 ):
     p, q = lax.axis_index("rows"), lax.axis_index("cols")
     me = p * COLS + q
-    chunks = [(1024 * t, min(1024, RAW_COLS - 1024 * t)) for t in range(5)]
+    def peer(k):
+        return (p ^ (k >> 2), q ^ (k & 3))
+
+    small = len(CHUNKS)
     loads = [
-        pltpu.make_async_copy(row_band_in, row_band, load_sem.at[5]),
-        pltpu.make_async_copy(col_band_in, col_band, load_sem.at[6]),
-        pltpu.make_async_copy(matrices_in, matrices, load_sem.at[7]),
-        pltpu.make_async_copy(twiddles_in, twiddles, load_sem.at[8]),
-        pltpu.make_async_copy(row_window_in.at[me], row_window, load_sem.at[9]),
-        pltpu.make_async_copy(col_window_in, col_window, load_sem.at[10]),
+        pltpu.make_async_copy(row_band_in.at[pl.ds(0, COLS * SLOT)], row_band, load_sem.at[small]),
+        pltpu.make_async_copy(col_band_in, col_band, load_sem.at[small + 1]),
+        pltpu.make_async_copy(matrices_in, matrices, load_sem.at[small + 2]),
+        pltpu.make_async_copy(floats_in.at[me], row_window, load_sem.at[small + 3]),
+        pltpu.make_async_copy(
+            floats_in.at[pl.ds(DEVICES, 2 + RADIX // 3)], common, load_sem.at[small + 4]
+        ),
     ]
     field_loads = [
         pltpu.make_async_copy(
-            field.at[0, :, pl.ds(begin, size)], raw.at[:, pl.ds(begin, size)], load_sem.at[t]
+            field.at[0, :, pl.ds(lo, hi - lo)], raw.at[:, pl.ds(lo, hi - lo)], load_sem.at[t]
         )
-        for t, (begin, size) in enumerate(chunks)
+        for t, (lo, hi) in enumerate(CHUNKS)
     ]
-    for copy in loads[:1] + field_loads[:1] + loads[1:2] + field_loads[1:] + loads[2:]:
+    for copy in loads[:1] + field_loads[:2] + loads[1:2]:
         copy.start()
 
+    def signal(semaphore, device):
+        pl.semaphore_signal(semaphore, inc=1, device_id=device, device_id_type=MESH)
+
     barrier = pltpu.get_barrier_semaphore()
-
-    @pl.loop(1, DEVICES)
-    def _(step):
-        other = (me + step) & (DEVICES - 1)
-        pl.semaphore_signal(
-            barrier, inc=1, device_id=(other >> 2, other & 3), device_id_type=MESH
-        )
+    for k in GROUP_C + GROUP_B + GROUP_A:
+        signal(barrier, peer(k))
+    for side, to_p in ((0, (p + 31) & 31), (3, (p + 1) & 31)):
+
+        @pl.when(q == side)
+        def _():
+            for to_q in range(COLS):
+                signal(barrier, (to_p, to_q))
+
+    for copy in field_loads[2:] + loads[2:]:
+        copy.start()
 
     for row in (HALF * SLOT, 256 + HALF * SLOT):
         turned[pl.ds(row, 256 - HALF * SLOT), :] = jnp.zeros((256 - HALF * SLOT, 256), jnp.float32)
     edges[...] = jnp.zeros_like(edges)
 
+    def row_copy(step, part, lo, size):
+        to = (q + step) & 3
+        return pltpu.make_async_remote_copy(
+            src_ref=cut.at[pl.ds(pl.multiple_of(to * SLOT, 8), SLOT), pl.ds(lo, size)],
+            dst_ref=gathered.at[q, :, pl.ds(lo, size)],
+            send_sem=near_send.at[step, part],
+            recv_sem=near_recv.at[q, part],
+            device_id=(p, to),
+            device_id_type=MESH,
+        )
+
+    def edge_copy(side, row):
+        return pltpu.make_async_remote_copy(
+            src_ref=cut.at[pl.ds((3 * SLOT, 0)[side] + RADIX + row, 1), :],
+            dst_ref=border.at[q, pl.ds(row, 1), :],
+            send_sem=edge_send.at[side, row],
+            recv_sem=edge_recv.at[q, row],
+            device_id=(((p + 1) & 31, 3 * 0), ((p + 31) & 31, 3))[side],
+            device_id_type=MESH,
+        )
+
+    early = [row_copy(step, 0, 0, 4 * LANES) for step in (2, 1, 3)]
+    late = [row_copy(step, 1, 4 * LANES, LANES) for step in (2, 1, 3)]
+    late += [edge_copy(side, row) for side in range(2) for row in range(2)]
+
     loads[0].wait()
-    for t, (begin, size) in enumerate(chunks):
+    for t, (begin, end) in enumerate(CHUNKS):
         field_loads[t].wait()
-        if t == 1:
-            loads[1].wait()
-        part = product(row_band[...], raw[:, begin : begin + size], ((1,), (0,)))
+        part = product(row_band[:, :RAW_ROWS], raw[:, begin:end], ((1,), (0,)))
         high, low = halves(part)
-        rowcut[: COLS * SLOT, begin : begin + size] = high
-        rowcut[COLS * SLOT :, begin : begin + size] = low
-        blocks = [] if t == 0 else ([t - 1, t] if t == 4 else [t - 1])
-        for u in blocks:
-            lo, hi = max(1024 * u - LANES, 0), min(1024 * u + 1024 + LANES, RAW_COLS)
+        rowcut[: COLS * SLOT, begin:end] = high
+        rowcut[COLS * SLOT :, begin:end] = low
+        for u in range(5):
+            if min(1024 * u + 1024 + LANES, RAW_COLS) != end:
+                continue
+            if u == 0:
+                loads[1].wait()
+            lo = max(1024 * u - LANES, 0)
             skip = lo - (1024 * u - LANES)
             both = product(
-                rowcut[:, lo:hi], col_band[skip : skip + hi - lo, :], ((1,), (0,))
+                rowcut[:, lo:end], col_band[skip : skip + end - lo, :], ((1,), (0,))
             )
             if u == 4:
                 both = both + product(
                     rowcut[:, :LANES], col_band[10 * LANES :, :], ((1,), (0,))
                 )
             cut[:, LANES * u : LANES * (u + 1)] = both[: COLS * SLOT] + both[COLS * SLOT :]
-
-    pl.semaphore_wait(barrier, DEVICES - 1)
-    near = []
-    for step in range(1, COLS):
-        to = (q + step) & 3
-        near.append(
-            pltpu.make_async_remote_copy(
-                src_ref=cut.at[pl.ds(pl.multiple_of(to * SLOT, 8), SLOT), :],
-                dst_ref=gathered.at[q],
-                send_sem=near_send.at[step - 1],
-                recv_sem=near_recv.at[q],
-                device_id=(p, to),
-                device_id_type=MESH,
-            )
-        )
-    for side, (row, to_p, to_q) in enumerate(
-        ((3 * SLOT + 16, (p + 1) & 31, 3 * 0), (16, (p + 31) & 31, 3))
-    ):
-        near.append(
-            pltpu.make_async_remote_copy(
-                src_ref=cut.at[pl.ds(row, 8), :],
-                dst_ref=border.at[q],
-                send_sem=near_send.at[3 + side],
-                recv_sem=edge_recv.at[q],
-                device_id=(to_p, to_q),
-                device_id_type=MESH,
-            )
-        )
-    for copy in near:
+            if u == 3:
+                pl.semaphore_wait(barrier, len(GROUP_A + GROUP_B + GROUP_C) + 2)
+                for k in GROUP_A:
+                    signal(group_ready, peer(k))
+                for copy in early:
+                    copy.start()
+    for copy in late:
         copy.start()
+    near = early + late
+    pl.semaphore_wait(group_ready, len(GROUP_A))
+    for k in GROUP_B:
+        signal(all_ready, peer(k))
     gathered[q] = cut[pl.ds(pl.multiple_of(q * SLOT, 8), SLOT), :]
     for copy in loads[2:]:
         copy.wait()
     for step in range(1, COLS):
         source = (q + step) & 3
-        pltpu.make_async_copy(
-            gathered.at[source],
-            gathered.at[source],
-            near_recv.at[source],
-        ).wait()
+        for part, (lo, size) in enumerate(((0, 4 * LANES), (4 * LANES, LANES))):
+            block = gathered.at[source, :, pl.ds(lo, size)]
+            pltpu.make_async_copy(block, block, near_recv.at[source, part]).wait()
 
     row_id = lax.broadcasted_iota(jnp.int32, (8, LANES), 0)
 
     @pl.when((q == 0) | (q == 3))
     def _():
         for source in range(COLS):
-            pltpu.make_async_copy(
-                border.at[source], border.at[source], edge_recv.at[source]
-            ).wait()
+            for row in range(2):
+                line = border.at[source, pl.ds(row, 1), :]
+                pltpu.make_async_copy(line, line, edge_recv.at[source, row]).wait()
         valid = ((q == 0) & (p > 0)) | ((q == 3) & (p < ROWS - 1))
         keep = jnp.where(valid, 2, 0)
         for t, tile in enumerate(joined([border[source] for source in range(COLS)])):
-            moved = pltpu.roll(tile, 6, 0)
-            edges[:, LANES * t : LANES * (t + 1)] = jnp.where(row_id < keep, moved, 0.0)
+            edges[:, LANES * t : LANES * (t + 1)] = jnp.where(row_id < keep, tile, 0.0)
 
     for s in range(3):
         rows = slice(8 * s, 8 * s + 8)
@@ -293,12 +313,12 @@
                 x + flag * edges[:, LANES * t : LANES * (t + 1)] for t, x in enumerate(points)
             ]
         points = [
-            x * row_window[rows, :] * col_window[:, LANES * t : LANES * (t + 1)]
+            x * row_window[rows, :] * common[2 + t // 3, 8 * (t % 3) : 8 * (t % 3) + 8, :]
             for t, x in enumerate(points)
         ]
         for freq, (real, imag) in enumerate(real_eighteen(points)):
             at = (freq // HALF) * 256 + (freq % HALF) * SLOT + 8 * s
-            cos, sin = twiddles[0, freq : freq + 1, :], twiddles[1, freq : freq + 1, :]
+            cos, sin = common[0, freq : freq + 1, :], common[1, freq : freq + 1, :]
             if imag is None:
                 turned[at : at + 8, :LANES] = real * cos
                 turned[at : at + 8, LANES:] = -real * sin
@@ -321,9 +341,9 @@
         lanes = pl.multiple_of((other & 1) * 256, 256)
         return leaving.at[:, pl.ds(other >> 1, 1), pl.ds(lanes, 256)]
 
-    @pl.loop(1, DEVICES)
-    def _(step):
-        other = (me + step) & (DEVICES - 1)
+    pl.semaphore_wait(all_ready, len(GROUP_B))
+    def far(k):
+        other = me ^ k
         pltpu.make_async_remote_copy(
             src_ref=block_of(other),
             dst_ref=arrived.at[:, pl.ds(me, 1), :],
@@ -332,6 +352,12 @@
             device_id=(other >> 2, other & 3),
             device_id_type=MESH,
         ).start()
+
+    for lo, hi in ((0, FARTHEST), (FARTHEST + 1, DEVICES)):
+
+        @pl.loop(lo, hi)
+        def _(step):
+            far(step ^ FARTHEST)
 
     pltpu.make_async_copy(block_of(me), arrived.at[:, pl.ds(me, 1), :], far_recv).start()
     pltpu.make_async_copy(arrived, arrived, far_recv).wait()
@@ -348,7 +374,7 @@
     for r in range(RADIX):
         real = mixed[0, pl.ds(r, HALF, stride=SLOT), :]
         imag = mixed[1, pl.ds(r, HALF, stride=SLOT), :]
-        cos, sin = twiddles[0, r : r + 1, :], twiddles[1, r : r + 1, :]
+        cos, sin = common[0, r : r + 1, :], common[1, r : r + 1, :]
         real_points.append(real * cos + imag * sin)
         imag_points.append(imag * cos - real * sin)
     for freq, (real, imag) in enumerate(complex_eighteen(real_points, imag_points)):
@@ -372,12 +398,11 @@
         out_specs=pl.BlockSpec(memory_space=pltpu.VMEM),
         scratch_shapes=[
             pltpu.VMEM((RAW_ROWS, RAW_COLS), bf16),
-            pltpu.VMEM(constants[0].shape, bf16),
+            pltpu.VMEM((COLS * SLOT, WIDE), bf16),
             pltpu.VMEM(constants[1].shape, bf16),
             pltpu.VMEM(constants[2].shape, bf16),
-            pltpu.VMEM(constants[3].shape, f32),
+            pltpu.VMEM((2 + RADIX // 3, SLOT, LANES), f32),
             pltpu.VMEM((SLOT, LANES), f32),
-            pltpu.VMEM(constants[5].shape, f32),
             pltpu.VMEM((2 * COLS * SLOT, RAW_COLS), bf16),
             pltpu.VMEM((COLS * SLOT, WIDE), f32),
             pltpu.VMEM((COLS, SLOT, WIDE), f32),
@@ -388,15 +413,18 @@
             pltpu.VMEM((2, DEVICES, 256), f32),
             pltpu.VMEM((2, 256, LANES), f32),
             pltpu.VMEM((DEVICES - 1, 4, LANES), f32),
-            pltpu.SemaphoreType.DMA((11,)),
-            pltpu.SemaphoreType.DMA((5,)),
-            pltpu.SemaphoreType.DMA((COLS,)),
-            pltpu.SemaphoreType.DMA((COLS,)),
+            pltpu.SemaphoreType.DMA((len(CHUNKS) + 5,)),
+            pltpu.SemaphoreType.DMA((COLS, 2)),
+            pltpu.SemaphoreType.DMA((COLS, 2)),
+            pltpu.SemaphoreType.DMA((2, 2)),
+            pltpu.SemaphoreType.DMA((COLS, 2)),
             pltpu.SemaphoreType.DMA,
             pltpu.SemaphoreType.DMA,
+            pltpu.SemaphoreType.REGULAR,
+            pltpu.SemaphoreType.REGULAR,
         ],
         compiler_params=pltpu.CompilerParams(
-            collective_id=0, has_side_effects=True, vmem_limit_bytes=56 * 2**20
+            collective_id=0, has_side_effects=True, vmem_limit_bytes=64 * 2**20 - 200 * 2**10
         ),
     )(field, *[jnp.asarray(c) for c in constants])
     return power[None]

time: 26.7 us -> 25.3 us (0.948)
  Pallas kernels: 25 us -> 23.5 us
    pallas_call x1, Pallas kernels: 25 us -> 23.5 us  [local(): pl.pallas_call(kernel, out_shape=jax.ShapeDtypeStruct((HALF, LENGTH), f32...]
where the time goes in v4:
time: 25.3 us; the launch traced here: 25.1 us
  Pallas kernels  23.5 us (93%)
  local copies, waits for them, and re-layouts  1.63 us (6%)
    pallas_call x1, Pallas kernels, local(): pl.pallas_call(kernel, out_shape=jax.ShapeDtypeStruct((HALF, LENGTH), f32...  23.5 us
    broadcast_in_dim x1, local copies, waits for them, and re-layouts, local(): return power[None]  1.63 us

profile of v4, /device:TPU:1, one launch (start us, length us, event | category | flops | bytes accessed | tf_op | source)
XLA Modules:
  0.0 25.1 jit_solution(5020883479784023927)
XLA Ops:
  0.0 23.5 %shard_map.55 = f32[9,2304]{1,0:T(8,128)} custom-call(bf16[1,576,4608]{2,1,0:T(8,128)(2,1)} %field.1, bf16[192,640]{1,0:T(8,128)(2,1)} %constant.8.clone.row_band_in, bf16[1408,128]{1,0:T(8,128)(2,1)} %constant.9.clone.col_band_in, bf16[768,256]{1,0:T(8,128)(2,1)} %constant.10.clone.matrices_in, f32[136,24,128]{2,1,0:T(8,128)} %constant.11.clone.floats_in), custom_call_target="tpu_custom_call" | custom-call | tf_op jit(solution)/shard_map/pallas_call | solution.py:394
  23.5 1.6 %copy.6 = f32[1,9,2304]{2,0,1:T(1,128)} copy(f32[1,9,2304]{2,1,0:T(8,128)} %bitcast.1) | data formatting | bytes 165888 | tf_op jit(solution)/shard_map/broadcast_in_dim | solution.py:430

commit v5 on v4

--- a/solution.py
+++ b/solution.py
@@ -424,7 +424,7 @@
             pltpu.SemaphoreType.REGULAR,
         ],
         compiler_params=pltpu.CompilerParams(
-            collective_id=0, has_side_effects=True, vmem_limit_bytes=64 * 2**20 - 200 * 2**10
+            collective_id=0, has_side_effects=True, vmem_limit_bytes=54936 * 2**10
         ),
     )(field, *[jnp.asarray(c) for c in constants])
     return power[None]

time: 25.3 us -> 23.7 us (0.937)
  local copies, waits for them, and re-layouts: 1.63 us -> 0.72 us
  Pallas kernels: 23.5 us -> 22.9 us
    broadcast_in_dim x1, local copies, waits for them, and re-layouts: 1.63 us -> 0.72 us  [local(): return power[None]]
    pallas_call x1, Pallas kernels: 23.5 us -> 22.9 us  [local(): pl.pallas_call(kernel, out_shape=jax.ShapeDtypeStruct((HALF, LENGTH), f32...]
where the time goes in v5:
time: 23.7 us; the launch traced here: 23.6 us
  Pallas kernels  22.9 us (97%)
  local copies, waits for them, and re-layouts  0.72 us (3%)
    pallas_call x1, Pallas kernels, local(): pl.pallas_call(kernel, out_shape=jax.ShapeDtypeStruct((HALF, LENGTH), f32...  22.9 us
    broadcast_in_dim x1, local copies, waits for them, and re-layouts, local(): return power[None]  0.72 us

profile of v5, /device:TPU:1, one launch (start us, length us, event | category | flops | bytes accessed | tf_op | source)
XLA Modules:
  0.0 23.6 jit_solution(6863958124193044132)
XLA Ops:
  0.0 22.9 %shard_map.55 = f32[9,2304]{1,0:T(8,128)S(1)} custom-call(bf16[1,576,4608]{2,1,0:T(8,128)(2,1)} %field.1, bf16[192,640]{1,0:T(8,128)(2,1)} %constant.8.clone.row_band_in, bf16[1408,128]{1,0:T(8,128)(2,1)} %constant.9.clone.col_band_in, bf16[768,256]{1,0:T(8,128)(2,1)} %constant.10.clone.matrices_in, f32[136,24,128]{2,1,0:T(8,128)} %constant.11.clone.floats_in), custom_call_target="tpu_custom_call" | custom-call | tf_op jit(solution)/shard_map/pallas_call | solution.py:394
  22.9 0.7 %copy.6 = f32[1,9,2304]{2,0,1:T(1,128)} copy(f32[1,9,2304]{2,1,0:T(8,128)S(1)} %bitcast.1) | data formatting | bytes 165888 | tf_op jit(solution)/shard_map/broadcast_in_dim | solution.py:430

commit v6 on v5

--- a/solution.py
+++ b/solution.py
@@ -26,10 +26,23 @@
 
 
 FARTHEST = 74
+NEARNESS = 2
+
+
+def bend(place):
+    return (place & 1) + 2 * ((place >> 1) & (1 - (place & 1)))
+
+
+def hops(device):
+    y = (device & 2) + ((device >> 4) & 1)
+    return bend((device >> 2) & 3) + bend((device >> 5) & 3) + bend(y)
+
+
+NEAR_ORIGIN = sorted((d for d in range(DEVICES) if hops(d) <= NEARNESS), key=hops)
 GROUP_A = [1, 2, 3]
 GROUP_B = [4 * k for k in range(1, 8)]
 GROUP_C = [32, 64, 96]
-CUTS = [0, 640] + [640 + 512 * t for t in range(1, 8)] + [RAW_COLS]
+CUTS = [0] + [LANES + 1024 * t for t in range(5)] + [RAW_COLS]
 CHUNKS = list(zip(CUTS[:-1], CUTS[1:]))
 
 
@@ -207,12 +220,17 @@
     barrier = pltpu.get_barrier_semaphore()
     for k in GROUP_C + GROUP_B + GROUP_A:
         signal(barrier, peer(k))
-    for side, to_p in ((0, (p + 31) & 31), (3, (p + 1) & 31)):
-
-        @pl.when(q == side)
-        def _():
-            for to_q in range(COLS):
-                signal(barrier, (to_p, to_q))
+    has_above, has_below = p > 0, p < ROWS - 1
+
+    @pl.when((q == 0) & has_above)
+    def _():
+        for to_q in range(COLS):
+            signal(barrier, (p - 1, to_q))
+
+    @pl.when((q == COLS - 1) & has_below)
+    def _():
+        for to_q in range(COLS):
+            signal(barrier, (p + 1, to_q))
 
     for copy in field_loads[2:] + loads[2:]:
         copy.start()
@@ -238,44 +256,64 @@
             dst_ref=border.at[q, pl.ds(row, 1), :],
             send_sem=edge_send.at[side, row],
             recv_sem=edge_recv.at[q, row],
-            device_id=(((p + 1) & 31, 3 * 0), ((p + 31) & 31, 3))[side],
+            device_id=((p + 1, 0), (p - 1, COLS - 1))[side],
             device_id_type=MESH,
         )
 
     early = [row_copy(step, 0, 0, 4 * LANES) for step in (2, 1, 3)]
     late = [row_copy(step, 1, 4 * LANES, LANES) for step in (2, 1, 3)]
-    late += [edge_copy(side, row) for side in range(2) for row in range(2)]
-
+    edge = [[edge_copy(side, row) for row in range(2)] for side in range(2)]
+
+    def filter_rows(begin, size):
+        part = product(row_band[:, :RAW_ROWS], raw[:, pl.ds(begin, size)], ((1,), (0,)))
+        high, low = halves(part)
+        rowcut[: COLS * SLOT, pl.ds(begin + LANES, size)] = high
+        rowcut[COLS * SLOT :, pl.ds(begin + LANES, size)] = low
+
+    rowcut[:, :LANES] = jnp.zeros((2 * COLS * SLOT, LANES), jnp.bfloat16)
     loads[0].wait()
-    for t, (begin, end) in enumerate(CHUNKS):
-        field_loads[t].wait()
-        part = product(row_band[:, :RAW_ROWS], raw[:, begin:end], ((1,), (0,)))
-        high, low = halves(part)
-        rowcut[: COLS * SLOT, begin:end] = high
-        rowcut[COLS * SLOT :, begin:end] = low
-        for u in range(5):
-            if min(1024 * u + 1024 + LANES, RAW_COLS) != end:
-                continue
-            if u == 0:
-                loads[1].wait()
-            lo = max(1024 * u - LANES, 0)
-            skip = lo - (1024 * u - LANES)
-            both = product(
-                rowcut[:, lo:end], col_band[skip : skip + end - lo, :], ((1,), (0,))
-            )
-            if u == 4:
-                both = both + product(
-                    rowcut[:, :LANES], col_band[10 * LANES :, :], ((1,), (0,))
-                )
-            cut[:, LANES * u : LANES * (u + 1)] = both[: COLS * SLOT] + both[COLS * SLOT :]
-            if u == 3:
-                pl.semaphore_wait(barrier, len(GROUP_A + GROUP_B + GROUP_C) + 2)
-                for k in GROUP_A:
-                    signal(group_ready, peer(k))
-                for copy in early:
-                    copy.start()
+    field_loads[0].wait()
+    filter_rows(0, LANES)
+    loads[1].wait()
+
+    @pl.loop(0, 4)
+    def _(u):
+        begin = pl.multiple_of(1024 * u, LANES)
+        chunk = raw.at[:, pl.ds(begin + LANES, 1024)]
+        pltpu.make_async_copy(chunk, chunk, load_sem.at[u + 1]).wait()
+        filter_rows(begin + LANES, 1024)
+        both = product(
+            rowcut[:, pl.ds(begin, 10 * LANES)], col_band[: 10 * LANES, :], ((1,), (0,))
+        )
+        cut[:, pl.ds(pl.multiple_of(LANES * u, LANES), LANES)] = (
+            both[: COLS * SLOT] + both[COLS * SLOT :]
+        )
+
+    pl.semaphore_wait(
+        barrier,
+        len(GROUP_A + GROUP_B + GROUP_C)
+        + has_above.astype(jnp.int32)
+        + has_below.astype(jnp.int32),
+    )
+    for k in GROUP_A:
+        signal(group_ready, peer(k))
+    for copy in early:
+        copy.start()
+    field_loads[5].wait()
+    filter_rows(CUTS[5], RAW_COLS - CUTS[5])
+    both = product(
+        rowcut[:, 4096 : RAW_COLS + LANES], col_band[: RAW_COLS + LANES - 4096, :], ((1,), (0,))
+    ) + product(rowcut[:, LANES : 2 * LANES], col_band[10 * LANES :, :], ((1,), (0,)))
+    cut[:, 4 * LANES :] = both[: COLS * SLOT] + both[COLS * SLOT :]
     for copy in late:
         copy.start()
+    for side, exists in enumerate((has_below, has_above)):
+
+        @pl.when(exists)
+        def _():
+            for copy in edge[side]:
+                copy.start()
+
     near = early + late
     pl.semaphore_wait(group_ready, len(GROUP_A))
     for k in GROUP_B:
@@ -291,59 +329,58 @@
 
     row_id = lax.broadcasted_iota(jnp.int32, (8, LANES), 0)
 
-    @pl.when((q == 0) | (q == 3))
+    @pl.when(((q == 0) & has_above) | ((q == COLS - 1) & has_below))
     def _():
         for source in range(COLS):
             for row in range(2):
                 line = border.at[source, pl.ds(row, 1), :]
                 pltpu.make_async_copy(line, line, edge_recv.at[source, row]).wait()
-        valid = ((q == 0) & (p > 0)) | ((q == 3) & (p < ROWS - 1))
-        keep = jnp.where(valid, 2, 0)
         for t, tile in enumerate(joined([border[source] for source in range(COLS)])):
-            edges[:, LANES * t : LANES * (t + 1)] = jnp.where(row_id < keep, tile, 0.0)
-
-    for s in range(3):
-        rows = slice(8 * s, 8 * s + 8)
+            edges[:, LANES * t : LANES * (t + 1)] = jnp.where(row_id < 2, tile, 0.0)
+
+    @pl.loop(0, 3)
+    def _(s):
+        rows = pl.ds(pl.multiple_of(8 * s, 8), 8)
         points = joined([gathered[source, rows, :] for source in range(COLS)])
-        if s == 2:
-            points = [jnp.where(row_id < 2, x, 0.0) for x in points]
-        if s != 1:
-            flag = jnp.where(q == (0 if s == 0 else 3), 1.0, 0.0).astype(jnp.float32)
-            points = [
-                x + flag * edges[:, LANES * t : LANES * (t + 1)] for t, x in enumerate(points)
-            ]
-        points = [
-            x * row_window[rows, :] * common[2 + t // 3, 8 * (t % 3) : 8 * (t % 3) + 8, :]
-            for t, x in enumerate(points)
-        ]
+        limit = jnp.where(s == 2, RADIX - 16, 8)
+        at_end = ((q == 0) & (s == 0)) | ((q == COLS - 1) & (s == 2))
+        flag = jnp.where(at_end, 1.0, 0.0).astype(jnp.float32)
+        mine = row_window[rows, :]
+        for t in range(RADIX):
+            point = jnp.where(row_id < limit, points[t], 0.0)
+            point = point + flag * edges[:, LANES * t : LANES * (t + 1)]
+            points[t] = point * mine * common[2 + t // 3, 8 * (t % 3) : 8 * (t % 3) + 8, :]
         for freq, (real, imag) in enumerate(real_eighteen(points)):
-            at = (freq // HALF) * 256 + (freq % HALF) * SLOT + 8 * s
+            at = (freq // HALF) * 256 + (freq % HALF) * SLOT
+            out = pl.ds(pl.multiple_of(at + 8 * s, 8), 8)
             cos, sin = common[0, freq : freq + 1, :], common[1, freq : freq + 1, :]
             if imag is None:
-                turned[at : at + 8, :LANES] = real * cos
-                turned[at : at + 8, LANES:] = -real * sin
+                turned[out, :LANES] = real * cos
+                turned[out, LANES:] = -real * sin
             else:
-                turned[at : at + 8, :LANES] = real * cos + imag * sin
-                turned[at : at + 8, LANES:] = imag * cos - real * sin
+                turned[out, :LANES] = real * cos + imag * sin
+                turned[out, LANES:] = imag * cos - real * sin
 
     first_high, first_low = matrices[:LANES, :], matrices[LANES : 2 * LANES, :]
-    for h in range(2):
-        high, low = halves(turned[256 * h : 256 * (h + 1), :])
+
+    @pl.loop(0, 2)
+    def _(h):
+        part = pl.ds(pl.multiple_of(256 * h, 256), 256)
+        high, low = halves(turned[part, :])
         both = (
             product(first_high, low, ((1,), (1,)))
             + product(first_low, high, ((1,), (1,)))
             + product(first_high, high, ((1,), (1,)))
         )
-        leaving[0, :, 256 * h : 256 * (h + 1)] = both[: LANES // 2]
-        leaving[1, :, 256 * h : 256 * (h + 1)] = both[LANES // 2 :]
+        leaving[0, :, part] = both[: LANES // 2]
+        leaving[1, :, part] = both[LANES // 2 :]
 
     def block_of(other):
         lanes = pl.multiple_of((other & 1) * 256, 256)
         return leaving.at[:, pl.ds(other >> 1, 1), pl.ds(lanes, 256)]
 
     pl.semaphore_wait(all_ready, len(GROUP_B))
-    def far(k):
-        other = me ^ k
+    def far(other):
         pltpu.make_async_remote_copy(
             src_ref=block_of(other),
             dst_ref=arrived.at[:, pl.ds(me, 1), :],
@@ -353,11 +390,19 @@
             device_id_type=MESH,
         ).start()
 
-    for lo, hi in ((0, FARTHEST), (FARTHEST + 1, DEVICES)):
-
-        @pl.loop(lo, hi)
-        def _(step):
-            far(step ^ FARTHEST)
+    for first in NEAR_ORIGIN:
+
+        @pl.when(me != first)
+        def _():
+            far(jnp.int32(first))
+
+    @pl.loop(0, DEVICES)
+    def _(step):
+        other = me ^ step ^ FARTHEST
+
+        @pl.when((hops(other) > NEARNESS) & (other != me))
+        def _():
+            far(other)
 
     pltpu.make_async_copy(block_of(me), arrived.at[:, pl.ds(me, 1), :], far_recv).start()
     pltpu.make_async_copy(arrived, arrived, far_recv).wait()
@@ -384,6 +429,13 @@
 
     for copy in near:
         copy.wait_send()
+    for side, exists in enumerate((has_below, has_above)):
+
+        @pl.when(exists)
+        def _():
+            for copy in edge[side]:
+                copy.wait_send()
+
     pltpu.make_async_copy(filler, filler, far_send).wait()
 
 
@@ -403,7 +455,7 @@
             pltpu.VMEM(constants[2].shape, bf16),
             pltpu.VMEM((2 + RADIX // 3, SLOT, LANES), f32),
             pltpu.VMEM((SLOT, LANES), f32),
-            pltpu.VMEM((2 * COLS * SLOT, RAW_COLS), bf16),
+            pltpu.VMEM((2 * COLS * SLOT, RAW_COLS + LANES), bf16),
             pltpu.VMEM((COLS * SLOT, WIDE), f32),
             pltpu.VMEM((COLS, SLOT, WIDE), f32),
             pltpu.VMEM((COLS, 8, WIDE), f32),

time: 23.7 us -> 22.9 us (0.966)
  Pallas kernels: 22.9 us -> 22.1 us
    pallas_call x1, Pallas kernels: 22.9 us -> 22.1 us  [local(): pl.pallas_call(kernel, out_shape=jax.ShapeDtypeStruct((HALF, LENGTH), f32...]
where the time goes in v6:
time: 22.9 us; the launch traced here: 22.8 us
  Pallas kernels  22.1 us (97%)
  local copies, waits for them, and re-layouts  0.72 us (3%)
    pallas_call x1, Pallas kernels, local(): pl.pallas_call(kernel, out_shape=jax.ShapeDtypeStruct((HALF, LENGTH), f32...  22.1 us
    broadcast_in_dim x1, local copies, waits for them, and re-layouts, local(): return power[None]  0.72 us

profile of v6, /device:TPU:1, one launch (start us, length us, event | category | flops | bytes accessed | tf_op | source)
XLA Modules:
  0.0 22.8 jit_solution(12628722866483007659)
XLA Ops:
  0.0 22.1 %shard_map.55 = f32[9,2304]{1,0:T(8,128)S(1)} custom-call(bf16[1,576,4608]{2,1,0:T(8,128)(2,1)} %field.1, bf16[192,640]{1,0:T(8,128)(2,1)} %constant.8.clone.row_band_in, bf16[1408,128]{1,0:T(8,128)(2,1)} %constant.9.clone.col_band_in, bf16[768,256]{1,0:T(8,128)(2,1)} %constant.10.clone.matrices_in, f32[136,24,128]{2,1,0:T(8,128)} %constant.11.clone.floats_in), custom_call_target="tpu_custom_call" | custom-call | tf_op jit(solution)/shard_map/pallas_call | solution.py:446
  22.1 0.7 %copy.6 = f32[1,9,2304]{2,0,1:T(1,128)} copy(f32[1,9,2304]{2,1,0:T(8,128)S(1)} %bitcast.1) | data formatting | bytes 165888 | tf_op jit(solution)/shard_map/broadcast_in_dim | solution.py:482

commit v7 on v6

v7 whole, which is shorter than its diff:
```python
import jax
import jax.numpy as jnp
import ml_dtypes
import numpy as np
from jax import lax
from jax.experimental import pallas as pl
from jax.experimental.pallas import tpu as pltpu
from jax.sharding import PartitionSpec as P

TAPS = 33
STRIDE = 8
REACH = TAPS // 2
MESH = pl.DeviceIdType.MESH

ROWS, COLS = 32, 4
DEVICES = ROWS * COLS
LENGTH = 2304
RADIX = LENGTH // DEVICES
RAW_ROWS = LENGTH * STRIDE // ROWS
RAW_COLS = LENGTH * STRIDE // COLS
OUT_COLS = RAW_COLS // STRIDE
CORES = 2
HOLD = CORES * RADIX
SLOT = 40
BLOCK = CORES * SLOT
PAIRS = DEVICES // CORES
LANES = 128
WIDE = 5 * LANES
HALF = RADIX // 2


FARTHEST = 74
NEARNESS = 2


def bend(place):
    return (place & 1) + 2 * ((place >> 1) & (1 - (place & 1)))


def hops(device):
    y = (device & 2) + ((device >> 4) & 1)
    return bend((device >> 2) & 3) + bend((device >> 5) & 3) + bend(y)


NEAR_ORIGIN = sorted((d for d in range(DEVICES) if hops(d) <= NEARNESS), key=hops)
GROUP_B = [4 * k for k in range(1, 8)]
GROUP_C = [low + 32 * z for z in (2, 1, 3, 0) for low in (2, 3, 0, 1) if low or z]
CUTS = [0] + [LANES + 1024 * t for t in range(5)] + [RAW_COLS]
CHUNKS = list(zip(CUTS[:-1], CUTS[1:]))


def taps_table():
    tap_ids = np.arange(TAPS, dtype=np.float32)
    shaped = np.sinc((tap_ids - np.float32(REACH)) / np.float32(STRIDE)).astype(np.float32)
    shaped = shaped * (
        np.float32(0.54)
        - np.float32(0.46) * np.cos(np.float32(2 * np.pi) * tap_ids / np.float32(TAPS - 1))
    )
    shaped = shaped / np.sum(shaped)
    return shaped.astype(ml_dtypes.bfloat16).astype(np.float32)


def tap_at(offset):
    taps = taps_table()
    inside = (offset >= 0) & (offset < TAPS)
    return np.where(inside, taps[np.clip(offset, 0, TAPS - 1)], 0).astype(ml_dtypes.bfloat16)


def split(matrix):
    high = matrix.astype(ml_dtypes.bfloat16)
    low = (matrix - high.astype(np.float64)).astype(ml_dtypes.bfloat16)
    return high, low


def tables():
    own = np.full((CORES, SLOT), -(10**6))
    own[:, :HOLD] = HOLD * np.arange(CORES)[:, None] + np.arange(HOLD)
    own[0, HOLD : HOLD + 2] = [-2, -1]
    own[1, HOLD : HOLD + 2] = [CORES * HOLD, CORES * HOLD + 1]
    raw = np.arange(RAW_ROWS)
    row_band = tap_at(raw[None, :] - STRIDE * own.reshape(-1, 1) + REACH)
    row_band = np.pad(row_band, ((0, 192 - BLOCK), (0, WIDE - RAW_ROWS)))

    lane = np.arange(LANES)
    inner = tap_at(np.arange(10 * LANES)[:, None] - LANES - STRIDE * lane[None, :] + REACH)
    edge = tap_at(lane[:, None] - STRIDE * (lane[None, :] - LANES) + REACH)
    col_band = np.concatenate([inner, edge], axis=0)

    def wave(places, count):
        angle = 2 * np.pi / LANES * (places[:, None] * np.arange(count)[None, :] % LANES)
        cos, sin = np.cos(angle), np.sin(angle)
        return np.block([[cos, -sin], [sin, cos]])

    pair = np.arange(PAIRS)
    first = np.concatenate(split(wave(lane, LANES // 2).T), axis=1)
    main = np.concatenate([wave(2 * pair + e, LANES) for e in range(2)], axis=1)
    odd = np.tile(pair % 2, 2)[:, None]
    before = wave(2 * pair - 1, LANES) * (1 - odd)
    after = wave(2 * pair + 2, LANES) * odd
    main_high, main_low = split(main)
    edge_high, edge_low = split(np.concatenate([before, after], axis=1))
    matrices = np.concatenate(
        [first, main_high, main_high, main_low, edge_high, edge_high, edge_low], axis=0
    )

    window = 0.5 - 0.5 * np.cos(2 * np.pi * np.arange(LENGTH) / LENGTH)
    held = own[pair % 2] + (HOLD * CORES) * (pair[:, None] // 2)
    inside = (held >= 0) & (held < LENGTH)
    row_window = np.where(inside, window[np.clip(held, 0, LENGTH - 1)], 0)
    row_window = np.broadcast_to(row_window.reshape(-1, 1), (PAIRS * SLOT, LANES))

    turn = 2 * np.pi / LENGTH * (np.arange(RADIX)[:, None] * lane[None, :])
    later = np.pad(np.stack([np.cos(turn), np.sin(turn)]), ((0, 0), (0, 24 - RADIX), (0, 0)))
    side_tables = []
    for side in range(2):
        sign = np.where(side * np.arange(24) % 2, -1.0, 1.0)[None, :, None]
        start = HALF * LANES * side
        block = window[start : start + HALF * LANES].reshape(HALF, LANES)
        weights = np.zeros((12, LANES))
        weights[:9] = block
        weights[4] = np.where(lane < 66, block[4], 0)
        weights[9] = np.where(lane >= 62, block[4], 0)
        if side == 0:
            weights[10, :2] = window[HALF * LANES : HALF * LANES + 2]
        else:
            weights[11, -2:] = window[HALF * LANES - 2 : HALF * LANES]
        weights = np.repeat(weights, 8, axis=0)
        side_tables.append((later * sign).reshape(-1, LANES))
        side_tables += [later.reshape(-1, LANES), weights]
    floats = np.concatenate([row_window] + side_tables, axis=0)
    return row_band, col_band, matrices, floats.astype(np.float32)


def real_nine(points):
    sums = [points[m] + points[9 - m] for m in range(1, 5)]
    gaps = [points[m] - points[9 - m] for m in range(1, 5)]
    reals, imags = [points[0] + sums[0] + sums[1] + sums[2] + sums[3]], [None]
    for freq in range(1, 5):
        real, imag = points[0], None
        for m in range(1, 5):
            phase = 2 * np.pi * (m * freq % 9) / 9
            real = real + sums[m - 1] * np.float32(np.cos(phase))
            term = gaps[m - 1] * np.float32(-np.sin(phase))
            imag = term if imag is None else imag + term
        reals.append(real)
        imags.append(imag)
    return reals, imags


def folded(points):
    evens = [points[2 * b % 18] for b in range(9)]
    odds = [points[(9 + 2 * b) % 18] for b in range(9)]
    sums, gaps = [], []
    for even, odd in zip(evens, odds):
        if odd is None:
            sums.append(even)
            gaps.append(even)
        elif even is None:
            sums.append(odd)
            gaps.append(-odd)
        else:
            sums.append(even + odd)
            gaps.append(even - odd)
    return real_nine(sums), real_nine(gaps)


def real_eighteen(points):
    both = folded(points)
    out = []
    for freq in range(18):
        reals, imags = both[freq % 2]
        at = freq % 9
        if at == 0:
            out.append((reals[0], None))
        elif at <= 4:
            out.append((reals[at], imags[at]))
        else:
            out.append((reals[9 - at], -imags[9 - at]))
    return out


def complex_eighteen(real_points, imag_points):
    both_real, both_imag = folded(real_points), folded(imag_points)
    out = []
    for freq in range(18):
        (a_re, a_im), (b_re, b_im) = both_real[freq % 2], both_imag[freq % 2]
        at = freq % 9
        if at == 0:
            out.append((a_re[0], b_re[0]))
        elif at <= 4:
            out.append((a_re[at] - b_im[at], a_im[at] + b_re[at]))
        else:
            out.append((a_re[9 - at] + b_im[9 - at], b_re[9 - at] - a_im[9 - at]))
    return out


def halves(value):
    high = value.astype(jnp.bfloat16)
    low = (value - high.astype(jnp.float32)).astype(jnp.bfloat16)
    return high, low


def product(left, right, dims):
    return lax.dot_general(left, right, (dims, ((), ())), preferred_element_type=jnp.float32)


def kernel(
    field, row_band_in, col_band_in, matrices_in, floats_in,
    power,
    raw, row_band, col_band, matrices, common, row_window,
    rowcut, cut, gathered, turned, leaving, arrived, mixed, beyond, filler,
    load_sem, near_send, near_recv, far_send, far_recv, all_ready,
):
    p, q = lax.axis_index("rows"), lax.axis_index("cols")
    me = p * COLS + q
    side, core = q >> 1, q & 1
    pair = p * CORES + core
    def peer(k):
        return (p ^ (k >> 2), q ^ (k & 3))

    small = len(CHUNKS)
    loads = [
        pltpu.make_async_copy(row_band_in.at[pl.ds(0, BLOCK)], row_band, load_sem.at[small]),
        pltpu.make_async_copy(col_band_in, col_band, load_sem.at[small + 1]),
        pltpu.make_async_copy(matrices_in, matrices, load_sem.at[small + 2]),
        pltpu.make_async_copy(
            floats_in.at[pl.ds(pl.multiple_of(pair * SLOT, 8), SLOT)],
            row_window,
            load_sem.at[small + 3],
        ),
        pltpu.make_async_copy(
            floats_in.at[pl.ds(pl.multiple_of(PAIRS * SLOT + side * 192, 8), 192)],
            common,
            load_sem.at[small + 4],
        ),
    ]
    field_loads = [
        pltpu.make_async_copy(
            field.at[0, :, pl.ds(lo, hi - lo)], raw.at[:, pl.ds(lo, hi - lo)], load_sem.at[t]
        )
        for t, (lo, hi) in enumerate(CHUNKS)
    ]
    for copy in loads[:1] + field_loads[:2] + loads[1:2]:
        copy.start()

    def signal(semaphore, device):
        pl.semaphore_signal(semaphore, inc=1, device_id=device, device_id_type=MESH)

    barrier = pltpu.get_barrier_semaphore()
    for k in GROUP_C + GROUP_B:
        signal(barrier, peer(k))
    for copy in field_loads[2:] + loads[2:]:
        copy.start()

    for row in (360, 384 + 360):
        turned[pl.ds(row, 24), :] = jnp.zeros((24, 256), jnp.float32)

    def row_copy(part, lo, size):
        to = 1 - core
        return pltpu.make_async_remote_copy(
            src_ref=cut.at[pl.ds(pl.multiple_of(to * SLOT, 8), SLOT), pl.ds(lo, size)],
            dst_ref=gathered.at[core, :, pl.ds(lo, size)],
            send_sem=near_send.at[part],
            recv_sem=near_recv.at[part],
            device_id=(p, q ^ 1),
            device_id_type=MESH,
        )

    near = [row_copy(0, 0, 4 * LANES), row_copy(1, 4 * LANES, LANES)]

    def filter_rows(begin, size):
        part = product(row_band[:, :RAW_ROWS], raw[:, pl.ds(begin, size)], ((1,), (0,)))
        high, low = halves(part)
        rowcut[: BLOCK, pl.ds(begin + LANES, size)] = high
        rowcut[BLOCK :, pl.ds(begin + LANES, size)] = low

    rowcut[:, :LANES] = jnp.zeros((2 * BLOCK, LANES), jnp.bfloat16)
    loads[0].wait()
    field_loads[0].wait()
    filter_rows(0, LANES)
    loads[1].wait()

    def step(u):
        begin = pl.multiple_of(1024 * u, LANES)
        chunk = raw.at[:, pl.ds(begin + LANES, 1024)]
        pltpu.make_async_copy(chunk, chunk, load_sem.at[u + 1]).wait()
        filter_rows(begin + LANES, 1024)
        both = product(
            rowcut[:, pl.ds(begin, 10 * LANES)], col_band[: 10 * LANES, :], ((1,), (0,))
        )
        cut[:, pl.ds(pl.multiple_of(LANES * u, LANES), LANES)] = (
            both[: BLOCK] + both[BLOCK :]
        )

    pl.loop(0, 3)(step)
    pl.semaphore_wait(barrier, len(GROUP_B + GROUP_C))
    for k in GROUP_B:
        signal(all_ready, peer(k))
    pl.loop(3, 4)(step)
    near[0].start()
    field_loads[5].wait()
    filter_rows(CUTS[5], RAW_COLS - CUTS[5])
    both = product(
        rowcut[:, 4096 : RAW_COLS + LANES], col_band[: RAW_COLS + LANES - 4096, :], ((1,), (0,))
    ) + product(rowcut[:, LANES : 2 * LANES], col_band[10 * LANES :, :], ((1,), (0,)))
    cut[:, 4 * LANES :] = both[: BLOCK] + both[BLOCK :]
    near[1].start()
    gathered[core] = cut[pl.ds(pl.multiple_of(core * SLOT, 8), SLOT), :]
    for copy in loads[2:]:
        copy.wait()
    for copy in near:
        copy.wait_recv()

    @pl.loop(0, SLOT // 8)
    def _(s):
        rows = pl.ds(pl.multiple_of(8 * s, 8), 8)
        mine = row_window[rows, :]
        left, right = gathered[0, rows, :], pltpu.roll(gathered[1, rows, :], 64, 1)

        def weighted(block, t, at):
            weight = common[96 + 8 * at : 104 + 8 * at, :]
            return block[:, LANES * t : LANES * (t + 1)] * mine * weight

        points = [None] * RADIX
        for t in range(4):
            points[t] = weighted(left, t, t)
            points[5 + t] = weighted(right, 1 + t, 5 + t)
        points[4] = weighted(left, 4, 4) + weighted(right, 0, 9)
        points[9] = weighted(right, 0, 10)
        points[17] = weighted(left, 4, 11)
        for freq, (real, imag) in enumerate(real_eighteen(points)):
            half, low = divmod(freq, HALF)
            at = 384 * half + jnp.where(s < 4, 32 * low + 8 * s, 288 + 8 * low)
            out = pl.ds(pl.multiple_of(at, 8), 8)
            cos, sin = common[freq : freq + 1, :], common[24 + freq : 25 + freq, :]
            if imag is None:
                turned[out, :LANES] = real * cos
                turned[out, LANES:] = -real * sin
            else:
                turned[out, :LANES] = real * cos + imag * sin
                turned[out, LANES:] = imag * cos - real * sin

    first_high, first_low = matrices[:LANES, :256], matrices[:LANES, 256:]

    @pl.loop(0, 2)
    def _(h):
        part = pl.ds(pl.multiple_of(384 * h, LANES), 384)
        high, low = halves(turned[part, :])
        both = (
            product(first_high, low, ((1,), (1,)))
            + product(first_low, high, ((1,), (1,)))
            + product(first_high, high, ((1,), (1,)))
        )
        leaving[0, :, part] = both[: LANES // 2]
        leaving[1, :, part] = both[LANES // 2 :]

    def block_of(other):
        lanes = pl.multiple_of((other & 1) * 384, LANES)
        return leaving.at[:, pl.ds(other >> 1, 1), pl.ds(lanes, 384)]

    landing = arrived.at[side, :, pl.ds(pair, 1), :]

    pl.semaphore_wait(all_ready, len(GROUP_B))
    def far(other):
        pltpu.make_async_remote_copy(
            src_ref=block_of(other),
            dst_ref=landing,
            send_sem=far_send,
            recv_sem=far_recv,
            device_id=(other >> 2, other & 3),
            device_id_type=MESH,
        ).start()

    for first in NEAR_ORIGIN:

        @pl.when(me != first)
        def _():
            far(jnp.int32(first))

    @pl.loop(0, DEVICES)
    def _(step):
        other = me ^ step ^ FARTHEST

        @pl.when((hops(other) > NEARNESS) & (other != me))
        def _():
            far(other)

    pltpu.make_async_copy(block_of(me), landing, far_recv).start()
    pltpu.make_async_copy(arrived, arrived, far_recv).wait()

    high, low = halves((arrived[0] + arrived[1]).reshape(2 * PAIRS, 384).T)
    both = jnp.concatenate([high, low], axis=1)
    total = product(both, matrices[128:384, :], ((1,), (0,))) + product(
        high, matrices[384:512, :], ((1,), (0,))
    )
    rest = product(both[288:360], matrices[512:768, :], ((1,), (0,))) + product(
        high[288:360], matrices[768:896, :], ((1,), (0,))
    )
    for t in range(4):
        mixed[t] = total[:, LANES * t : LANES * (t + 1)]
        beyond[t] = rest[:, LANES * t : LANES * (t + 1)]

    def held(e, part, slot):
        if slot < 32:
            return mixed[2 * e + part, pl.ds(slot, HALF, stride=32), :]
        return mixed[2 * e + part, pl.ds(288 + slot - 32, HALF, stride=8), :]

    real_points, imag_points = [], []
    for r in range(RADIX):
        real, imag = (held(0, part, r) + held(1, part, RADIX + r) for part in range(2))
        if r < 2:
            real = real + beyond[2, pl.ds(4 + r, HALF, stride=8), :]
            imag = imag + beyond[3, pl.ds(4 + r, HALF, stride=8), :]
        if r >= RADIX - 2:
            real = real + beyond[0, pl.ds(4 + r - (RADIX - 2), HALF, stride=8), :]
            imag = imag + beyond[1, pl.ds(4 + r - (RADIX - 2), HALF, stride=8), :]
        cos, sin = common[48 + r : 49 + r, :], common[72 + r : 73 + r, :]
        real_points.append(real * cos + imag * sin)
        imag_points.append(imag * cos - real * sin)
    for freq, (real, imag) in enumerate(complex_eighteen(real_points, imag_points)):
        power[:, LANES * freq : LANES * (freq + 1)] = (real * real + imag * imag) * np.float32(
            8.0 / (LENGTH * LENGTH)
        )

    for copy in near:
        copy.wait_send()
    pltpu.make_async_copy(filler, filler, far_send).wait()


def local(field):
    constants = tables()
    anywhere = pl.BlockSpec(memory_space=pltpu.HBM)
    f32, bf16 = jnp.float32, jnp.bfloat16
    power = pl.pallas_call(
        kernel,
        out_shape=jax.ShapeDtypeStruct((HALF, LENGTH), f32),
        in_specs=[anywhere] * (1 + len(constants)),
        out_specs=pl.BlockSpec(memory_space=pltpu.VMEM),
        scratch_shapes=[
            pltpu.VMEM((RAW_ROWS, RAW_COLS), bf16),
            pltpu.VMEM((BLOCK, WIDE), bf16),
            pltpu.VMEM(constants[1].shape, bf16),
            pltpu.VMEM(constants[2].shape, bf16),
            pltpu.VMEM((192, LANES), f32),
            pltpu.VMEM((SLOT, LANES), f32),
            pltpu.VMEM((2 * BLOCK, RAW_COLS + LANES), bf16),
            pltpu.VMEM((BLOCK, WIDE), f32),
            pltpu.VMEM((CORES, SLOT, WIDE), f32),
            pltpu.VMEM((768, 256), f32),
            pltpu.VMEM((2, LANES // 2, 768), f32),
            pltpu.VMEM((2, 2, PAIRS, 384), f32),
            pltpu.VMEM((4, 384, LANES), f32),
            pltpu.VMEM((4, 72, LANES), f32),
            pltpu.VMEM((DEVICES - 1, 6, LANES), f32),
            pltpu.SemaphoreType.DMA((len(CHUNKS) + 5,)),
            pltpu.SemaphoreType.DMA((2,)),
            pltpu.SemaphoreType.DMA((2,)),
            pltpu.SemaphoreType.DMA,
            pltpu.SemaphoreType.DMA,
            pltpu.SemaphoreType.REGULAR,
        ],
        compiler_params=pltpu.CompilerParams(
            collective_id=0, has_side_effects=True, vmem_limit_bytes=54936 * 2**10
        ),
    )(field, *[jnp.asarray(c) for c in constants])
    return power[None]


def solution(mesh):
    return jax.shard_map(
        local,
        mesh=mesh,
        in_specs=(P(None, "rows", "cols"),),
        out_specs=P(None, ("rows", "cols"), None),
        check_vma=False,
    )
```

time: 22.9 us -> 19.9 us (0.87)
  Pallas kernels: 22.1 us -> 19.1 us
    pallas_call x1, Pallas kernels: 22.1 us -> 19.1 us  [local(): pl.pallas_call(kernel, out_shape=jax.ShapeDtypeStruct((HALF, LENGTH), f32...]
where the time goes in v7:
time: 19.9 us; the launch traced here: 19.8 us
  Pallas kernels  19.1 us (96%)
  local copies, waits for them, and re-layouts  0.72 us (4%)
    pallas_call x1, Pallas kernels, local(): pl.pallas_call(kernel, out_shape=jax.ShapeDtypeStruct((HALF, LENGTH), f32...  19.1 us
    broadcast_in_dim x1, local copies, waits for them, and re-layouts, local(): return power[None]  0.72 us

profile of v7, /device:TPU:1, one launch (start us, length us, event | category | flops | bytes accessed | tf_op | source)
XLA Modules:
  0.0 19.8 jit_solution(13763148092423650617)
XLA Ops:
  0.0 19.1 %shard_map.55 = f32[9,2304]{1,0:T(8,128)S(1)} custom-call(bf16[1,576,4608]{2,1,0:T(8,128)(2,1)} %field.1, bf16[192,640]{1,0:T(8,128)(2,1)} %constant.8.clone.row_band_in, bf16[1408,128]{1,0:T(8,128)(2,1)} %constant.9.clone.col_band_in, bf16[896,512]{1,0:T(8,128)(2,1)} %constant.10.clone.matrices_in, f32[2944,128]{1,0:T(8,128)} %constant.11.clone.floats_in), custom_call_target="tpu_custom_call" | custom-call | tf_op jit(solution)/shard_map/pallas_call | solution.py:434
  19.1 0.7 %copy.6 = f32[1,9,2304]{2,0,1:T(1,128)} copy(f32[1,9,2304]{2,1,0:T(8,128)S(1)} %bitcast.1) | data formatting | bytes 165888 | tf_op jit(solution)/shard_map/broadcast_in_dim | solution.py:466

commit v8 on v7

--- a/solution.py
+++ b/solution.py
@@ -240,7 +240,7 @@
         )
         for t, (lo, hi) in enumerate(CHUNKS)
     ]
-    for copy in loads[:1] + field_loads[:2] + loads[1:2]:
+    for copy in loads[:1] + field_loads[:2] + loads[1:2] + field_loads[2:]:
         copy.start()
 
     def signal(semaphore, device):
@@ -249,8 +249,6 @@
     barrier = pltpu.get_barrier_semaphore()
     for k in GROUP_C + GROUP_B:
         signal(barrier, peer(k))
-    for copy in field_loads[2:] + loads[2:]:
-        copy.start()
 
     for row in (360, 384 + 360):
         turned[pl.ds(row, 24), :] = jnp.zeros((24, 256), jnp.float32)
@@ -293,6 +291,8 @@
         )
 
     pl.loop(0, 3)(step)
+    for copy in loads[2:]:
+        copy.start()
     pl.semaphore_wait(barrier, len(GROUP_B + GROUP_C))
     for k in GROUP_B:
         signal(all_ready, peer(k))
@@ -330,8 +330,7 @@
         points[17] = weighted(left, 4, 11)
         for freq, (real, imag) in enumerate(real_eighteen(points)):
             half, low = divmod(freq, HALF)
-            at = 384 * half + jnp.where(s < 4, 32 * low + 8 * s, 288 + 8 * low)
-            out = pl.ds(pl.multiple_of(at, 8), 8)
+            out = pl.ds(pl.multiple_of(384 * half + 72 * s + 8 * low, 8), 8)
             cos, sin = common[freq : freq + 1, :], common[24 + freq : 25 + freq, :]
             if imag is None:
                 turned[out, :LANES] = real * cos
@@ -361,6 +360,7 @@
     landing = arrived.at[side, :, pl.ds(pair, 1), :]
 
     pl.semaphore_wait(all_ready, len(GROUP_B))
+
     def far(other):
         pltpu.make_async_remote_copy(
             src_ref=block_of(other),
@@ -390,20 +390,21 @@
 
     high, low = halves((arrived[0] + arrived[1]).reshape(2 * PAIRS, 384).T)
     both = jnp.concatenate([high, low], axis=1)
-    total = product(both, matrices[128:384, :], ((1,), (0,))) + product(
-        high, matrices[384:512, :], ((1,), (0,))
-    )
+    for e in range(2):
+        rows, lanes = slice(144 * e, 144 * e + 216), slice(256 * e, 256 * e + 256)
+        total = product(both[rows], matrices[128:384, lanes], ((1,), (0,))) + product(
+            high[rows], matrices[384:512, lanes], ((1,), (0,))
+        )
+        mixed[2 * e], mixed[2 * e + 1] = total[:, :LANES], total[:, LANES:]
     rest = product(both[288:360], matrices[512:768, :], ((1,), (0,))) + product(
         high[288:360], matrices[768:896, :], ((1,), (0,))
     )
     for t in range(4):
-        mixed[t] = total[:, LANES * t : LANES * (t + 1)]
         beyond[t] = rest[:, LANES * t : LANES * (t + 1)]
 
     def held(e, part, slot):
-        if slot < 32:
-            return mixed[2 * e + part, pl.ds(slot, HALF, stride=32), :]
-        return mixed[2 * e + part, pl.ds(288 + slot - 32, HALF, stride=8), :]
+        row = 72 * (slot // 8) + slot % 8 - 144 * e
+        return mixed[2 * e + part, pl.ds(row, HALF, stride=8), :]
 
     real_points, imag_points = [], []
     for r in range(RADIX):
@@ -449,7 +450,7 @@
             pltpu.VMEM((768, 256), f32),
             pltpu.VMEM((2, LANES // 2, 768), f32),
             pltpu.VMEM((2, 2, PAIRS, 384), f32),
-            pltpu.VMEM((4, 384, LANES), f32),
+            pltpu.VMEM((4, 216, LANES), f32),
             pltpu.VMEM((4, 72, LANES), f32),
             pltpu.VMEM((DEVICES - 1, 6, LANES), f32),
             pltpu.SemaphoreType.DMA((len(CHUNKS) + 5,)),

time: 19.9 us -> 19.7 us (0.990)
  Pallas kernels: 19.1 us -> 18.8 us
    pallas_call x1, Pallas kernels: 19.1 us -> 18.8 us  [local(): pl.pallas_call(kernel, out_shape=jax.ShapeDtypeStruct((HALF, LENGTH), f32...]
where the time goes in v8:
time: 19.7 us; the launch traced here: 19.6 us
  Pallas kernels  18.8 us (95%)
  local copies, waits for them, and re-layouts  0.72 us (4%)
    pallas_call x1, Pallas kernels, local(): pl.pallas_call(kernel, out_shape=jax.ShapeDtypeStruct((HALF, LENGTH), f32...  18.8 us
    broadcast_in_dim x1, local copies, waits for them, and re-layouts, local(): return power[None]  0.72 us

profile of v8, /device:TPU:1, one launch (start us, length us, event | category | flops | bytes accessed | tf_op | source)
XLA Modules:
  0.0 19.6 jit_solution(14886985887781737756)
XLA Ops:
  0.0 18.8 %shard_map.55 = f32[9,2304]{1,0:T(8,128)S(1)} custom-call(bf16[1,576,4608]{2,1,0:T(8,128)(2,1)} %field.1, bf16[192,640]{1,0:T(8,128)(2,1)} %constant.8.clone.row_band_in, bf16[1408,128]{1,0:T(8,128)(2,1)} %constant.9.clone.col_band_in, bf16[896,512]{1,0:T(8,128)(2,1)} %constant.10.clone.matrices_in, f32[2944,128]{1,0:T(8,128)} %constant.11.clone.floats_in), custom_call_target="tpu_custom_call" | custom-call | tf_op jit(solution)/shard_map/pallas_call | solution.py:435
  18.8 0.7 %copy.6 = f32[1,9,2304]{2,0,1:T(1,128)} copy(f32[1,9,2304]{2,1,0:T(8,128)S(1)} %bitcast.1) | data formatting | bytes 165888 | tf_op jit(solution)/shard_map/broadcast_in_dim | solution.py:467

commit v9 on v8

--- a/solution.py
+++ b/solution.py
@@ -311,7 +311,7 @@
     for copy in near:
         copy.wait_recv()
 
-    @pl.loop(0, SLOT // 8)
+    @pl.loop(0, SLOT // 8, unroll=True)
     def _(s):
         rows = pl.ds(pl.multiple_of(8 * s, 8), 8)
         mine = row_window[rows, :]
@@ -341,9 +341,8 @@
 
     first_high, first_low = matrices[:LANES, :256], matrices[:LANES, 256:]
 
-    @pl.loop(0, 2)
-    def _(h):
-        part = pl.ds(pl.multiple_of(384 * h, LANES), 384)
+    def spread(h):
+        part = slice(384 * h, 384 * (h + 1))
         high, low = halves(turned[part, :])
         both = (
             product(first_high, low, ((1,), (1,)))
@@ -358,8 +357,6 @@
         return leaving.at[:, pl.ds(other >> 1, 1), pl.ds(lanes, 384)]
 
     landing = arrived.at[side, :, pl.ds(pair, 1), :]
-
-    pl.semaphore_wait(all_ready, len(GROUP_B))
 
     def far(other):
         pltpu.make_async_remote_copy(
@@ -371,11 +368,17 @@
             device_id_type=MESH,
         ).start()
 
-    for first in NEAR_ORIGIN:
-
-        @pl.when(me != first)
-        def _():
-            far(jnp.int32(first))
+    for h in (1, 0):
+        spread(h)
+        if h == 1:
+            pl.semaphore_wait(all_ready, len(GROUP_B))
+        for first in NEAR_ORIGIN:
+            if first % 2 != h:
+                continue
+
+            @pl.when(me != first)
+            def _():
+                far(jnp.int32(first))
 
     @pl.loop(0, DEVICES)
     def _(step):
@@ -419,7 +422,7 @@
         real_points.append(real * cos + imag * sin)
         imag_points.append(imag * cos - real * sin)
     for freq, (real, imag) in enumerate(complex_eighteen(real_points, imag_points)):
-        power[:, LANES * freq : LANES * (freq + 1)] = (real * real + imag * imag) * np.float32(
+        power[:, 0, LANES * freq : LANES * (freq + 1)] = (real * real + imag * imag) * np.float32(
             8.0 / (LENGTH * LENGTH)
         )
 
@@ -434,7 +437,7 @@
     f32, bf16 = jnp.float32, jnp.bfloat16
     power = pl.pallas_call(
         kernel,
-        out_shape=jax.ShapeDtypeStruct((HALF, LENGTH), f32),
+        out_shape=jax.ShapeDtypeStruct((HALF, 1, LENGTH), f32),
         in_specs=[anywhere] * (1 + len(constants)),
         out_specs=pl.BlockSpec(memory_space=pltpu.VMEM),
         scratch_shapes=[
@@ -464,7 +467,7 @@
             collective_id=0, has_side_effects=True, vmem_limit_bytes=54936 * 2**10
         ),
     )(field, *[jnp.asarray(c) for c in constants])
-    return power[None]
+    return power.reshape(1, HALF, LENGTH)
 
 
 def solution(mesh):

time: 19.7 us -> 19.6 us (level)
  the two profiles are of different devices: /device:TPU:1 before, /device:TPU:0 now
where the time goes in v9:
time: 19.6 us; the launch traced here: 19.5 us
  Pallas kernels  18.9 us (96%)
  local copies, waits for them, and re-layouts  0.64 us (3%)
    pallas_call x1, Pallas kernels, local(): pl.pallas_call(kernel, out_shape=jax.ShapeDtypeStruct((HALF, 1, LENGTH),...  18.9 us
    unnamed x1, local copies, waits for them, and re-layouts  0.64 us

profile of v9, /device:TPU:0, one launch (start us, length us, event | category | flops | bytes accessed | tf_op | source)
XLA Modules:
  0.0 19.5 jit_solution(13661433869929559412)
XLA Ops:
  0.0 18.9 %shard_map.55 = f32[9,1,2304]{2,1,0:T(1,128)S(1)} custom-call(bf16[1,576,4608]{2,1,0:T(8,128)(2,1)} %field.1, bf16[192,640]{1,0:T(8,128)(2,1)} %constant.8.clone.row_band_in, bf16[1408,128]{1,0:T(8,128)(2,1)} %constant.9.clone.col_band_in, bf16[896,512]{1,0:T(8,128)(2,1)} %constant.10.clone.matrices_in, f32[2944,128]{1,0:T(8,128)} %constant.11.clone.floats_in), custom_call_target="tpu_custom_call" | custom-call | tf_op jit(solution)/shard_map/pallas_call | solution.py:438
  18.9 0.6 %copy.7 = f32[1,9,2304]{2,0,1:T(1,128)} copy(f32[1,9,2304]{2,0,1:T(1,128)S(1)} %bitcast.1) | data formatting | bytes 165888
